TPU v7x, 512 devices: a whole 4x8x8 slice. The times are simulated.
512 devices in a mesh: visit: 8 (over z), strip: 64 (over y, x, core).
Axes of the slice: x: 4, y: 8, z: 8, core: 2. Of those that a mesh axis runs over, the one named last changes fastest.
Arguments:
- template: bfloat16 [2048, 1024], P('strip', 'visit'), may hold values from -60 to 60
- science_src: bfloat16 [8, 4096, 1024], P('visit', 'strip'), may hold values from -180 to 180
- target_rows: int32 [8, 4096], P('visit'), may hold values from 0 to 2047, as said below
- row_taps: bfloat16 [45, 21], replicated, may hold values from -1.25 to 1.25
- col_taps: bfloat16 [45, 21], replicated, may hold values from -1.25 to 1.25
Outputs:
- difference: float32 [8, 2048, 1024], P('visit', 'strip')
- kernel_coeffs: float32 [8, 45], P('visit')
Inputs may be any that keep to these rules, and one draw needn't show every extreme that they name: `target_rows`: row j of a visit lies on strip device j // 64; its target's strip is target // 32. Of the 64 rows of one strip device at most 2 target the same strip, and in every visit one strip receives exactly 2 rows from every strip device.
All inputs are finite; a program needn't handle non-finite values.
Results may differ from a plain program's by a relative error of at most 0.0014.
Values may be sent and summed in bfloat16 or wider, within the bound.
No kernel may reach another device: no remote copies, remote signals or barrier semaphores. Data moves between devices by JAX's collectives and lax.ppermute only.
A program may use at most 64 MiB of HBM per device.

v0:
```python
import jax
import jax.numpy as jnp
from jax import lax
from jax.sharding import PartitionSpec as P


def with_halo(cells, sides, width):
    for axis, dim in sides:
        count = lax.axis_size(axis)
        ends = count - 1
        head = lax.slice_in_dim(cells, 0, width, axis=dim)
        tail = lax.slice_in_dim(cells, cells.shape[dim] - width, cells.shape[dim], axis=dim)
        cells = jnp.concatenate(
            [
                lax.ppermute(tail, axis, [(i, (i + 1) % count) for i in range(ends)]),
                cells,
                lax.ppermute(head, axis, [((i + 1) % count, i) for i in range(ends)]),
            ],
            axis=dim,
        )
    return cells


def convolve(framed, row_taps, col_taps):
    tap_count = col_taps.shape[1]
    margin = (tap_count - 1) // 2
    basis_count = col_taps.shape[0]
    height = framed.shape[0]
    out_width = framed.shape[1] - 2 * margin
    block_cols = 128
    block_pad = 64
    extra_pad = block_pad - margin
    widened = jnp.pad(framed, ((0, 0), (extra_pad, extra_pad)))
    blocks = out_width // block_cols
    window_cols = block_cols + 2 * block_pad
    pieces = widened.reshape(height, blocks + 1, block_cols)
    windows = jnp.concatenate([pieces[:, :-1], pieces[:, 1:]], axis=2)
    tap_index = jnp.arange(window_cols)[:, None] - jnp.arange(block_cols)[None, :] - extra_pad
    band_table = jnp.zeros((window_cols, basis_count, block_cols), jnp.float32)
    for t in range(tap_count):
        band_table = band_table + jnp.where(
            (tap_index == t)[:, None, :], col_taps[:, t].astype(jnp.float32)[None, :, None], 0.0
        )
    band_table = band_table.astype(jnp.bfloat16).reshape(window_cols, basis_count * block_cols)
    smoothed = jnp.dot(
        windows.reshape(height * blocks, window_cols),
        band_table,
        preferred_element_type=jnp.float32,
    )
    smoothed = smoothed.astype(jnp.bfloat16).reshape(height, blocks, basis_count, block_cols)
    smoothed = jnp.transpose(smoothed, (2, 0, 1, 3)).reshape(basis_count, height, out_width)
    out_rows = height - 2 * margin
    row_lag = jnp.arange(height)[None, :] - jnp.arange(out_rows)[:, None]
    row_band = jnp.zeros((basis_count, out_rows, height), jnp.float32)
    for t in range(tap_count):
        row_band = row_band + jnp.where(
            (row_lag == t)[None, :, :], row_taps[:, t].astype(jnp.float32)[:, None, None], 0.0
        )
    row_band = row_band.astype(jnp.bfloat16)
    basis = jnp.einsum("krs,ksw->krw", row_band, smoothed, preferred_element_type=jnp.float32)
    return basis.astype(jnp.bfloat16)


def split_three(values):
    upper = values.astype(jnp.bfloat16)
    rest = values - upper.astype(jnp.float32)
    middle = rest.astype(jnp.bfloat16)
    lower = (rest - middle.astype(jnp.float32)).astype(jnp.bfloat16)
    return jnp.stack([upper, middle, lower])


def body(template, science_src, target_rows, row_taps, col_taps):
    tap_count = row_taps.shape[1]
    margin = (tap_count - 1) // 2
    basis_count = row_taps.shape[0]
    strips = lax.axis_size("strip")
    visits = lax.axis_size("visit")
    rows_dev = template.shape[0]
    part_width = template.shape[1]
    full_width = part_width * visits
    src_dev = science_src.shape[1]
    capacity = max(2, 2 * src_dev // strips)
    my_strip = lax.axis_index("strip")
    targets = target_rows[0].reshape(strips, src_dev)
    dest_strip = targets // rows_dev
    row_order = jnp.arange(src_dev, dtype=jnp.int32)
    shared_dest = (dest_strip[:, :, None] == dest_strip[:, None, :]) & (
        row_order[:, None] < row_order[None, :]
    )[None]
    arrival = jnp.sum(shared_dest.astype(jnp.int32), axis=1)
    send_slot = dest_strip * capacity + arrival
    my_slots = lax.dynamic_index_in_dim(send_slot, my_strip, 0, keepdims=False)
    slot_ids = jnp.arange(strips * capacity, dtype=jnp.int32)
    placer = (my_slots[None, :] == slot_ids[:, None]).astype(jnp.bfloat16)
    outgoing = jnp.dot(placer, science_src[0], preferred_element_type=jnp.float32).astype(
        jnp.bfloat16
    )
    outgoing = outgoing.reshape(strips, capacity, full_width)
    incoming = lax.all_to_all(outgoing, "strip", split_axis=0, concat_axis=0, tiled=True)
    anchor = (jnp.arange(strips, dtype=jnp.int32) * capacity)[:, None] + arrival
    aimed_here = dest_strip == my_strip
    local_row = targets - my_strip * rows_dev
    slot_hit = (aimed_here[..., None] & (anchor[..., None] == slot_ids)).reshape(
        strips * src_dev, strips * capacity
    )
    row_hit = (local_row[..., None] == jnp.arange(rows_dev, dtype=jnp.int32)).reshape(
        strips * src_dev, rows_dev
    )
    spread = lax.dot_general(
        row_hit.astype(jnp.bfloat16),
        slot_hit.astype(jnp.bfloat16),
        (((0,), (0,)), ((), ())),
        preferred_element_type=jnp.float32,
    )
    spread = spread.astype(jnp.bfloat16)
    science = jnp.dot(
        spread, incoming.reshape(strips * capacity, full_width), preferred_element_type=jnp.float32
    )
    rimmed = with_halo(template, (("strip", 0),), margin)
    gathered = lax.all_gather(rimmed, "visit", axis=1, tiled=True)
    framed = jnp.pad(gathered, ((0, 0), (margin, margin)))
    basis = convolve(framed, row_taps, col_taps)
    basis_flat = basis.reshape(basis_count, rows_dev * full_width)
    science_parts = split_three(science.reshape(rows_dev * full_width))
    moment_parts = lax.dot_general(
        science_parts, basis_flat, (((1,), (1,)), ((), ())), preferred_element_type=jnp.float32
    )
    moment_part = jnp.sum(moment_parts, axis=0)
    gram_part = lax.dot_general(
        basis_flat, basis_flat, (((1,), (1,)), ((), ())), preferred_element_type=jnp.float32
    )
    gram_total, moment = lax.psum((gram_part, moment_part), "strip")
    factor = jnp.linalg.cholesky(gram_total)
    forward = lax.linalg.triangular_solve(factor, moment[:, None], left_side=True, lower=True)
    answer = lax.linalg.triangular_solve(
        factor, forward, left_side=True, lower=True, transpose_a=True
    )
    kernel_coeffs = answer[:, 0]
    coeff_parts = split_three(kernel_coeffs)
    model_parts = jnp.dot(coeff_parts, basis_flat, preferred_element_type=jnp.float32)
    model = jnp.sum(model_parts, axis=0).reshape(rows_dev, full_width)
    difference = science - model
    return (difference[None], kernel_coeffs[None])


def solution(mesh):
    in_specs = (P("strip", "visit"), P("visit", "strip", None), P("visit", None), P(), P())
    out_specs = (P("visit", "strip", None), P("visit", None))
    return jax.shard_map(body, mesh=mesh, in_specs=in_specs, out_specs=out_specs, check_vma=False)
```

profile of v0, /device:TPU:32, one launch (start us, length us, event | category | flops | bytes accessed | tf_op | source)
XLA Modules:
  0.0 381.0 jit_solution(10450472504711623824)
XLA Ops:
  0.6 0.0 copy-start
  0.7 1.4 fusion.145
  2.0 1.9 collective-permute-start
  3.9 7.0 %collective-permute-start.1 = (bf16[10,128]{1,0:T(8,128)(2,1)}, bf16[10,128]{1,0:T(8,128)(2,1)S(1)}, u32[]{:S(2)}, u32[]{:S(2)}) collective-permute-start(bf16[10,128]{1,0:T(8,128)(2,1)} %get-tuple-element.11), channel_id=1, source_target_pairs={{1,0},{2,1},{3,2},{4,3},{5,4},{6,5},{7,6},{8,7},{9,8},{10,9},{11,1... | collective-permute-start | bytes 7688 | tf_op jit(solution)/shard_map/ppermute | solution.py:17
  10.9 0.5 broadcast.1378
  11.4 1.4 reduce.9
  12.8 0.1 reshape_squeeze.3
  12.9 0.6 broadcast_compare_fusion
  13.5 0.7 convert_reduce_fusion
  14.3 0.2 convolution_convert_fusion.1
  14.5 0.8 reshape.1494
  15.3 7.9 %all-to-all-start = ((bf16[64,2,1024]{2,1,0:T(2,128)(2,1)}), bf16[64,2,1024]{2,1,0:T(2,128)(2,1)S(1)}, u32[]{:S(2)}, u32[]{:S(2)}) async-start(bf16[64,2,1024]{2,1,0:T(2,128)(2,1)} %reshape.1494), calls=%async_computation | async-start | bytes 524288 | tf_op jit(solution)/shard_map/all_to_all | solution.py:99
  23.3 0.6 fusion.86
  23.9 0.7 fusion.88
  24.6 0.6 fusion.90
  25.2 0.6 fusion.92
  25.9 0.6 fusion.94
  26.5 0.6 fusion.96
  27.2 0.6 fusion.98
  27.8 1.6 bitcast_convert_fusion.20
  29.5 1.3 bitcast_convert_fusion.1
  30.8 0.6 fusion.100
  31.4 0.6 fusion.109
  32.0 0.6 fusion.111
  32.6 0.6 fusion.113
  33.2 0.6 fusion.115
  33.8 0.6 fusion.117
  34.4 0.6 fusion.119
  35.0 0.6 fusion.121
  35.6 0.6 fusion.123
  36.2 0.6 fusion.125
  36.8 0.6 fusion.127
  37.4 1.6 bitcast_convert_fusion.41
  39.1 1.3 bitcast_convert_fusion.22
  40.4 0.7 broadcast_add_fusion
  41.1 0.6 broadcast_subtract_fusion
  41.7 11.8 %add_convert_fusion = bf16[256,45,128]{0,2,1:T(8,128)(2,1)S(1)} fusion(f32[45]{0:T(128)} %get-tuple-element.53, f32[45]{0:T(128)} %get-tuple-element.52, f32[45]{0:T(128)} %get-tuple-element.34, f32[45]{0:T(128)} %get-tuple-element.35, f32[45]{0:T(128)} %get-tuple-element.36, f32[45]{0:T(128)} %get-tuple-element.37, f32[45]{0:T(128)} %get-tuple-element.38, ...), kind=kLoop, calls=%fused_computation.1 | loop fusion | flops 61931520 | bytes 3641028 | tf_op jit(solution)/shard_map/convert_element_type | solution.py:44
  53.5 0.6 fusion.129
  54.1 0.0 collective-permute-done
  54.1 27.6 %all_gather.3 = bf16[52,1024]{1,0:T(8,128)(2,1)S(1)} all-gather(bf16[52,128]{1,0:T(8,128)(2,1)S(1)} %pad_maximum_fusion), channel_id=1, replica_groups=mesh['visit'=8,'strip'=64] {'visit'}, dimensions={1}, use_global_device_ids=true | all-gather | bytes 119808 | tf_op jit(solution)/shard_map/all_gather | solution.py:120
  81.7 0.8 pad.21
  82.4 1.0 reshape.1496
  83.5 3.7 fusion.4
  87.6 8.5 %reshape.1499 = bf16[45,52,1024]{2,0,1:T(8,128)(2,1)} reshape(bf16[45,52,8,128]{3,2,0,1:T(8,128)(2,1)} %fusion.4) | data formatting | bytes 9584640 | tf_op jit(solution)/shard_map/reshape | solution.py:51
  96.5 13.3 %fusion.5 = bf16[45,32,1024]{2,1,0:T(8,128)(2,1)S(1)} fusion(bf16[45,52,1024]{2,0,1:T(8,128)(2,1)} %reshape.1499, f32[45]{0:T(128)} %get-tuple-element.32, f32[45]{0:T(128)} %get-tuple-element.31, f32[45]{0:T(128)S(1)} %copy-done.25, f32[45]{0:T(128)S(1)} %copy-done.26, f32[45]{0:T(128)S(1)} %copy-done.27, f32[45]{0:T(128)S(1)} %copy-done.28, ...), kind=kOutput, calls=%fused_computation.7 | convolution fusion | flops 157973760 | bytes 7780164 | tf_op jit(solution)/shard_map/krs,ksw->krw/dot_general | solution.py:60
  109.7 0.5 pad.22
  110.3 1.9 copy.25
  112.1 6.8 %fusion.11 = f32[45,45]{0,1:T(8,128)} fusion(bf16[45,32,1024]{2,1,0:T(8,128)(2,1)S(1)} %fusion.5), kind=kOutput, calls=%fused_computation.14 | convolution fusion | flops 132710400 | bytes 2957220 | tf_op jit(solution)/shard_map/dot_general | solution.py:129
  118.9 0.8 reshape.1495
  119.7 2.5 fusion.21
  122.2 0.1 copy.24
  122.4 0.2 fusion.130
  122.5 0.1 convert_element_type.631
  122.6 1.0 convolution_reduce_fusion.1
  123.6 246.7 %all-reduce.2 = (f32[45,45]{0,1:T(8,128)S(1)}, f32[45]{0:T(128)S(1)}) all-reduce(f32[45,45]{0,1:T(8,128)} %fusion.11, f32[45]{0:T(128)S(1)} %convolution_reduce_fusion.1), channel_id=1, replica_groups=mesh['visit'=8,'strip'=64] {'strip'}, use_global_device_ids=true, to_apply=%region_1.2 | all-reduce | flops 2070 | bytes 16560 | tf_op jit(solution)/shard_map/psum | solution.py:132
  370.3 0.1 copy.21
  370.4 4.1 %cholesky.16 = f32[45,45]{1,0:T(8,128)S(1)} custom-call(f32[45,45]{1,0:T(8,128)S(1)} %fusion.108), custom_call_target="Cholesky" | custom-call | tf_op jit(solution)/shard_map/jit(cholesky)/cholesky | solution.py:133
  374.6 0.6 compare_reduce_fusion
  375.2 0.7 fusion.104
  375.9 3.4 custom-call.8
  379.3 0.2 convolution_bitcast_fusion
  379.5 0.2 fusion.105
  379.7 0.6 convolution_reduce_fusion
  380.3 0.7 subtract_bitcast_fusion
  (101 shorter events, 0.4 us)
Async XLA Ops:
  0.6 13.6 %copy-start = (bf16[1,64,1024]{2,1,0:T(8,128)(2,1)S(1)}, bf16[1,64,1024]{2,1,0:T(8,128)(2,1)}, u32[]{:S(2)}) copy-start(bf16[1,64,1024]{2,1,0:T(8,128)(2,1)} %param.6) | copy-start | bytes 393220
  0.6 53.5 %copy-start.1 = (bf16[32,128]{1,0:T(8,128)(2,1)S(1)}, bf16[32,128]{1,0:T(8,128)(2,1)}, u32[]{:S(2)}) copy-start(bf16[32,128]{1,0:T(8,128)(2,1)} %param.5) | copy-start | bytes 24580
  2.0 52.1 %collective-permute-start = (bf16[10,128]{1,0:T(8,128)(2,1)}, bf16[10,128]{1,0:T(8,128)(2,1)S(1)}, u32[]{:S(2)}, u32[]{:S(2)}) collective-permute-start(bf16[10,128]{1,0:T(8,128)(2,1)} %get-tuple-element.10), channel_id=1, source_target_pairs={{0,1},{1,2},{2,3},{3,4},{4,5},{5,6},{6,7},{7,8},{8,9},{9,10},{10,1... | collective-permute-start | bytes 7688 | tf_op jit(solution)/shard_map/ppermute | solution.py:15
  3.9 50.2 %collective-permute-start.1 = (bf16[10,128]{1,0:T(8,128)(2,1)}, bf16[10,128]{1,0:T(8,128)(2,1)S(1)}, u32[]{:S(2)}, u32[]{:S(2)}) collective-permute-start(bf16[10,128]{1,0:T(8,128)(2,1)} %get-tuple-element.11), channel_id=1, source_target_pairs={{1,0},{2,1},{3,2},{4,3},{5,4},{6,5},{7,6},{8,7},{9,8},{10,9},{11,1... | collective-permute-start | bytes 7688 | tf_op jit(solution)/shard_map/ppermute | solution.py:17
  15.3 103.6 %all-to-all-start = ((bf16[64,2,1024]{2,1,0:T(2,128)(2,1)}), bf16[64,2,1024]{2,1,0:T(2,128)(2,1)S(1)}, u32[]{:S(2)}, u32[]{:S(2)}) async-start(bf16[64,2,1024]{2,1,0:T(2,128)(2,1)} %reshape.1494), calls=%async_computation | async-start | bytes 524288 | tf_op jit(solution)/shard_map/all_to_all | solution.py:99
  87.2 8.9 %copy-start.3 = (pred[32,52]{1,0:T(8,128)(4,1)S(1)}, pred[32,52]{1,0:T(8,128)(4,1)}, u32[]{:S(2)}) copy-start(pred[32,52]{1,0:T(8,128)(4,1)} %get-tuple-element.77) | copy-start | bytes 4996
  87.2 8.9 %copy-start.4 = (pred[32,52]{1,0:T(8,128)(4,1)S(1)}, pred[32,52]{1,0:T(8,128)(4,1)}, u32[]{:S(2)}) copy-start(pred[32,52]{1,0:T(8,128)(4,1)} %get-tuple-element.78) | copy-start | bytes 4996
  87.2 8.9 %copy-start.5 = (pred[32,52]{1,0:T(8,128)(4,1)S(1)}, pred[32,52]{1,0:T(8,128)(4,1)}, u32[]{:S(2)}) copy-start(pred[32,52]{1,0:T(8,128)(4,1)} %get-tuple-element.79) | copy-start | bytes 4996
  87.2 8.9 %copy-start.6 = (pred[32,52]{1,0:T(8,128)(4,1)S(1)}, pred[32,52]{1,0:T(8,128)(4,1)}, u32[]{:S(2)}) copy-start(pred[32,52]{1,0:T(8,128)(4,1)} %get-tuple-element.80) | copy-start | bytes 4996
  87.2 8.9 %copy-start.7 = (pred[32,52]{1,0:T(8,128)(4,1)S(1)}, pred[32,52]{1,0:T(8,128)(4,1)}, u32[]{:S(2)}) copy-start(pred[32,52]{1,0:T(8,128)(4,1)} %get-tuple-element.81) | copy-start | bytes 4996
  87.2 8.9 %copy-start.8 = (pred[32,52]{1,0:T(8,128)(4,1)S(1)}, pred[32,52]{1,0:T(8,128)(4,1)}, u32[]{:S(2)}) copy-start(pred[32,52]{1,0:T(8,128)(4,1)} %get-tuple-element.82) | copy-start | bytes 4996
  87.2 8.9 %copy-start.9 = (pred[32,52]{1,0:T(8,128)(4,1)S(1)}, pred[32,52]{1,0:T(8,128)(4,1)}, u32[]{:S(2)}) copy-start(pred[32,52]{1,0:T(8,128)(4,1)} %get-tuple-element.83) | copy-start | bytes 4996
  87.2 8.9 %copy-start.10 = (pred[32,52]{1,0:T(8,128)(4,1)S(1)}, pred[32,52]{1,0:T(8,128)(4,1)}, u32[]{:S(2)}) copy-start(pred[32,52]{1,0:T(8,128)(4,1)} %get-tuple-element.84) | copy-start | bytes 4996
  87.2 8.9 %copy-start.11 = (pred[32,52]{1,0:T(8,128)(4,1)S(1)}, pred[32,52]{1,0:T(8,128)(4,1)}, u32[]{:S(2)}) copy-start(pred[32,52]{1,0:T(8,128)(4,1)} %get-tuple-element.85) | copy-start | bytes 4996
  87.3 8.9 %copy-start.12 = (pred[32,52]{1,0:T(8,128)(4,1)S(1)}, pred[32,52]{1,0:T(8,128)(4,1)}, u32[]{:S(2)}) copy-start(pred[32,52]{1,0:T(8,128)(4,1)} %get-tuple-element.86) | copy-start | bytes 4996
  87.3 8.9 %copy-start.13 = (pred[32,52]{1,0:T(8,128)(4,1)S(1)}, pred[32,52]{1,0:T(8,128)(4,1)}, u32[]{:S(2)}) copy-start(pred[32,52]{1,0:T(8,128)(4,1)} %get-tuple-element.87) | copy-start | bytes 4996
  87.3 8.9 %copy-start.14 = (pred[32,52]{1,0:T(8,128)(4,1)S(1)}, pred[32,52]{1,0:T(8,128)(4,1)}, u32[]{:S(2)}) copy-start(pred[32,52]{1,0:T(8,128)(4,1)} %get-tuple-element.88) | copy-start | bytes 4996
  87.3 8.9 %copy-start.15 = (pred[32,52]{1,0:T(8,128)(4,1)S(1)}, pred[32,52]{1,0:T(8,128)(4,1)}, u32[]{:S(2)}) copy-start(pred[32,52]{1,0:T(8,128)(4,1)} %get-tuple-element.89) | copy-start | bytes 4996
  87.3 8.9 %copy-start.16 = (pred[32,52]{1,0:T(8,128)(4,1)S(1)}, pred[32,52]{1,0:T(8,128)(4,1)}, u32[]{:S(2)}) copy-start(pred[32,52]{1,0:T(8,128)(4,1)} %get-tuple-element.90) | copy-start | bytes 4996
  87.3 8.9 %copy-start.17 = (pred[32,52]{1,0:T(8,128)(4,1)S(1)}, pred[32,52]{1,0:T(8,128)(4,1)}, u32[]{:S(2)}) copy-start(pred[32,52]{1,0:T(8,128)(4,1)} %get-tuple-element.91) | copy-start | bytes 4996
  87.3 8.9 %copy-start.18 = (pred[32,52]{1,0:T(8,128)(4,1)S(1)}, pred[32,52]{1,0:T(8,128)(4,1)}, u32[]{:S(2)}) copy-start(pred[32,52]{1,0:T(8,128)(4,1)} %get-tuple-element.92) | copy-start | bytes 4996
  87.3 8.9 %copy-start.19 = (pred[32,52]{1,0:T(8,128)(4,1)S(1)}, pred[32,52]{1,0:T(8,128)(4,1)}, u32[]{:S(2)}) copy-start(pred[32,52]{1,0:T(8,128)(4,1)} %get-tuple-element.93) | copy-start | bytes 4996
  87.3 8.9 %copy-start.20 = (pred[32,52]{1,0:T(8,128)(4,1)S(1)}, pred[32,52]{1,0:T(8,128)(4,1)}, u32[]{:S(2)}) copy-start(pred[32,52]{1,0:T(8,128)(4,1)} %get-tuple-element.94) | copy-start | bytes 4996
  87.3 8.9 %copy-start.21 = (pred[32,52]{1,0:T(8,128)(4,1)S(1)}, pred[32,52]{1,0:T(8,128)(4,1)}, u32[]{:S(2)}) copy-start(pred[32,52]{1,0:T(8,128)(4,1)} %get-tuple-element.95) | copy-start | bytes 4996
  87.4 8.9 %copy-start.22 = (pred[32,52]{1,0:T(8,128)(4,1)S(1)}, pred[32,52]{1,0:T(8,128)(4,1)}, u32[]{:S(2)}) copy-start(pred[32,52]{1,0:T(8,128)(4,1)} %get-tuple-element.96) | copy-start | bytes 4996
  87.4 8.9 %copy-start.23 = (pred[32,52]{1,0:T(8,128)(4,1)S(1)}, pred[32,52]{1,0:T(8,128)(4,1)}, u32[]{:S(2)}) copy-start(pred[32,52]{1,0:T(8,128)(4,1)} %fusion.129) | copy-start | bytes 4996
  87.4 8.9 %copy-start.24 = (f32[45]{0:T(128)S(1)}, f32[45]{0:T(128)}, u32[]{:S(2)}) copy-start(f32[45]{0:T(128)} %get-tuple-element.12) | copy-start | bytes 544
  87.4 8.9 %copy-start.25 = (f32[45]{0:T(128)S(1)}, f32[45]{0:T(128)}, u32[]{:S(2)}) copy-start(f32[45]{0:T(128)} %get-tuple-element.13) | copy-start | bytes 544
  87.4 8.9 %copy-start.26 = (f32[45]{0:T(128)S(1)}, f32[45]{0:T(128)}, u32[]{:S(2)}) copy-start(f32[45]{0:T(128)} %get-tuple-element.14) | copy-start | bytes 544
  87.4 8.9 %copy-start.27 = (f32[45]{0:T(128)S(1)}, f32[45]{0:T(128)}, u32[]{:S(2)}) copy-start(f32[45]{0:T(128)} %get-tuple-element.15) | copy-start | bytes 544
  87.4 8.9 %copy-start.28 = (f32[45]{0:T(128)S(1)}, f32[45]{0:T(128)}, u32[]{:S(2)}) copy-start(f32[45]{0:T(128)} %get-tuple-element.16) | copy-start | bytes 544
  87.4 8.9 %copy-start.29 = (f32[45]{0:T(128)S(1)}, f32[45]{0:T(128)}, u32[]{:S(2)}) copy-start(f32[45]{0:T(128)} %get-tuple-element.17) | copy-start | bytes 544
  87.4 8.9 %copy-start.30 = (f32[45]{0:T(128)S(1)}, f32[45]{0:T(128)}, u32[]{:S(2)}) copy-start(f32[45]{0:T(128)} %get-tuple-element.18) | copy-start | bytes 544
  87.4 8.9 %copy-start.31 = (f32[45]{0:T(128)S(1)}, f32[45]{0:T(128)}, u32[]{:S(2)}) copy-start(f32[45]{0:T(128)} %get-tuple-element.19) | copy-start | bytes 544
  87.5 8.9 %copy-start.32 = (f32[45]{0:T(128)S(1)}, f32[45]{0:T(128)}, u32[]{:S(2)}) copy-start(f32[45]{0:T(128)} %get-tuple-element.20) | copy-start | bytes 544
  87.5 8.9 %copy-start.33 = (f32[45]{0:T(128)S(1)}, f32[45]{0:T(128)}, u32[]{:S(2)}) copy-start(f32[45]{0:T(128)} %get-tuple-element.21) | copy-start | bytes 544
  87.5 8.9 %copy-start.34 = (f32[45]{0:T(128)S(1)}, f32[45]{0:T(128)}, u32[]{:S(2)}) copy-start(f32[45]{0:T(128)} %get-tuple-element.22) | copy-start | bytes 544
  87.5 8.9 %copy-start.35 = (f32[45]{0:T(128)S(1)}, f32[45]{0:T(128)}, u32[]{:S(2)}) copy-start(f32[45]{0:T(128)} %get-tuple-element.23) | copy-start | bytes 544
  87.5 8.9 %copy-start.36 = (f32[45]{0:T(128)S(1)}, f32[45]{0:T(128)}, u32[]{:S(2)}) copy-start(f32[45]{0:T(128)} %get-tuple-element.24) | copy-start | bytes 544
  87.5 8.9 %copy-start.37 = (f32[45]{0:T(128)S(1)}, f32[45]{0:T(128)}, u32[]{:S(2)}) copy-start(f32[45]{0:T(128)} %get-tuple-element.25) | copy-start | bytes 544
  87.5 8.9 %copy-start.38 = (f32[45]{0:T(128)S(1)}, f32[45]{0:T(128)}, u32[]{:S(2)}) copy-start(f32[45]{0:T(128)} %get-tuple-element.26) | copy-start | bytes 544
  87.5 8.9 %copy-start.39 = (f32[45]{0:T(128)S(1)}, f32[45]{0:T(128)}, u32[]{:S(2)}) copy-start(f32[45]{0:T(128)} %get-tuple-element.27) | copy-start | bytes 544
  87.5 8.9 %copy-start.40 = (f32[45]{0:T(128)S(1)}, f32[45]{0:T(128)}, u32[]{:S(2)}) copy-start(f32[45]{0:T(128)} %get-tuple-element.28) | copy-start | bytes 544
  87.5 8.9 %copy-start.41 = (f32[45]{0:T(128)S(1)}, f32[45]{0:T(128)}, u32[]{:S(2)}) copy-start(f32[45]{0:T(128)} %get-tuple-element.29) | copy-start | bytes 544
  87.6 8.9 %copy-start.42 = (f32[45]{0:T(128)S(1)}, f32[45]{0:T(128)}, u32[]{:S(2)}) copy-start(f32[45]{0:T(128)} %get-tuple-element.30) | copy-start | bytes 544
  110.3 9.4 %copy-start.2 = (pred[64,64]{1,0:T(8,128)(4,1)S(1)}, pred[64,64]{1,0:T(8,128)(4,1)}, u32[]{:S(2)}) copy-start(pred[64,64]{1,0:T(8,128)(4,1)} %get-tuple-element.4) | copy-start | bytes 12292
  379.6 1.3 copy-start.43
where the time goes:
time: 382 us; the launch traced here: 381 us
  blocking collectives  274 us (72%)
  other arithmetic  43.5 us (11%)
  matrix products  28.3 us (7%)
  local copies, waits for them, and re-layouts  16.7 us (4%)
  starting transfers between devices  16.7 us (4%)
    psum x1, blocking collectives, body(): gram_total, moment = lax.psum((gram_part, moment_part), 'strip')  247 us
    all_gather x1, blocking collectives, body(): gathered = lax.all_gather(rimmed, 'visit', axis=1, tiled=True)  27.6 us
    dot_general x1, matrix products, convolve(): jnp.einsum('krs,ksw->krw', row_band, smoothed, preferred_element_type=jnp...  13.3 us
    convert_element_type x1, other arithmetic, convolve(): band_table.astype(jnp.bfloat16)  11.8 us
    reshape x1, local copies, waits for them, and re-layouts, convolve(): jnp.transpose(smoothed, (2, 0, 1, 3))  8.52 us
    all_to_all x1, starting transfers between devices, body(): lax.all_to_all(outgoing, 'strip', split_axis=0, concat_axis=0, tiled=True)  7.86 us
  transfers between devices with their start and end apart: 3, of which 0 were waited for; matrix products, arithmetic and copies ran while one was open for 19% of the time, Pallas kernels for 0%

commit v1 on v0

v1 whole, which is shorter than its diff:
```python
import jax
import jax.numpy as jnp
from jax import lax
from jax.experimental import pallas as pl
from jax.experimental.pallas import tpu as pltpu
from jax.sharding import Mesh, PartitionSpec as P

STRIPS = 64
VISITS = 8
ROWS = 32
COLS = 1024
LANES = 128
SRC = 64
TAPS = 21
REACH = 10
NB = 45
PAD = 48
HALO = 16
FRAME = ROWS + 2 * HALO
QUAD = 4
SUB = 8
BIG = 1 << 20
F32 = jnp.float32
BF16 = jnp.bfloat16
STRIP = ("y", "x", "core")


def vmem(count):
    return [pl.BlockSpec(memory_space=pltpu.VMEM)] * count


def iota(shape, dim):
    return lax.broadcasted_iota(jnp.int32, shape, dim)


def send_kernel(mine_ref, src_ref, out_ref):
    dest = mine_ref[...] // ROWS
    at_dest = dest == iota((STRIPS, SRC), 0)
    order = iota((STRIPS, SRC), 1)
    first = jnp.min(jnp.where(at_dest, order, BIG), axis=1, keepdims=True)
    last = jnp.max(jnp.where(at_dest, order, -1), axis=1, keepdims=True)
    src = src_ref[...]
    one = at_dest & (order == first)
    two = at_dest & (order == last) & (last != first)
    for slot, pick in enumerate((one, two)):
        rows = jnp.dot(pick.astype(F32).astype(BF16), src, preferred_element_type=F32)
        out_ref[:, slot * COLS:(slot + 1) * COLS] = rows.astype(BF16)


def basis_kernel(tile_ref, row_ref, col_ref, basis_ref, gram_ref, win_ref, wide_ref):
    zero = jnp.zeros((FRAME, LANES // 2), BF16)
    blocks = [tile_ref[b] for b in range(VISITS)]
    halves = [zero]
    for b in range(VISITS):
        halves += [blocks[b][:, :LANES // 2], blocks[b][:, LANES // 2:]]
    halves.append(zero)
    shifted = [jnp.concatenate([halves[2 * i], halves[2 * i + 1]], axis=1) for i in range(VISITS + 1)]
    for b in range(VISITS):
        win_ref[b * FRAME:(b + 1) * FRAME, :LANES] = shifted[b]
        win_ref[b * FRAME:(b + 1) * FRAME, LANES:] = shifted[b + 1]
    above = iota((LANES, LANES), 1) <= iota((LANES, LANES), 0) - (LANES // 2 - REACH)

    def quad(q, carry):
        smooth = []
        bands = []
        for pair in range(QUAD // 2):
            tops, bottoms = [], []
            for j in range(2):
                k = q * QUAD + pair * 2 + j
                taps = jnp.broadcast_to(col_ref[pl.ds(k, 1), :], (LANES, LANES))
                wheel = pltpu.roll(taps, 0, 1, stride=1, stride_axis=0)
                tops.append(jnp.where(above, wheel, 0.0).astype(BF16))
                bottoms.append(jnp.where(above, 0.0, wheel).astype(BF16))
            band = jnp.concatenate(
                [jnp.concatenate(tops, axis=1), jnp.concatenate(bottoms, axis=1)], axis=0
            )
            both = jnp.dot(win_ref[...], band, preferred_element_type=F32).astype(BF16)
            smooth += [both[:, :LANES], both[:, LANES:]]
        for j in range(QUAD):
            k = q * QUAD + j
            taps = jnp.broadcast_to(row_ref[pl.ds(k, 1), :], (ROWS, LANES))
            band = pltpu.roll(taps, (j % 2) * FRAME, 1, stride=1, stride_axis=0).astype(BF16)
            blank = jnp.zeros((ROWS, LANES), BF16)
            bands.append(jnp.concatenate([band, blank] if j < 2 else [blank, band], axis=1))
        row_band = jnp.concatenate(bands, axis=0)
        for b in range(0, VISITS, 2):
            stack = jnp.concatenate(
                [
                    jnp.concatenate(
                        [s[b * FRAME:(b + 1) * FRAME], s[(b + 1) * FRAME:(b + 2) * FRAME]], axis=1
                    )
                    for s in smooth
                ],
                axis=0,
            )
            done = jnp.dot(row_band, stack, preferred_element_type=F32)
            for j in range(QUAD):
                for half in range(2):
                    wide_ref[b + half, pl.ds(q * QUAD + j, ROWS, stride=PAD), :] = done[
                        j * ROWS:(j + 1) * ROWS, half * LANES:(half + 1) * LANES
                    ]
        return carry

    lax.fori_loop(0, PAD // QUAD, quad, 0)

    def gram_step(r, total):
        at = pl.multiple_of(r * PAD, PAD)
        images = jnp.concatenate(
            [wide_ref[b, pl.ds(at, PAD), :].astype(BF16) for b in range(VISITS)], axis=1
        )
        basis_ref[pl.ds(at, PAD), :] = images
        return total + lax.dot_general(
            images, images, (((1,), (1,)), ((), ())), preferred_element_type=F32
        )

    gram_ref[...] = lax.fori_loop(0, ROWS, gram_step, jnp.zeros((PAD, PAD), F32))


def moment_kernel(me_ref, targets_ref, got_ref, basis_ref, gram_ref, science_ref, part_ref):
    targets = targets_ref[...]
    here = targets // ROWS == me_ref[0]
    key = iota((STRIPS, SRC), 1) * ROWS + targets % ROWS
    first = jnp.min(jnp.where(here, key, BIG), axis=1, keepdims=True)
    last = jnp.max(jnp.where(here, key, -1), axis=1, keepdims=True)
    rows = iota((STRIPS, ROWS), 1)
    one = (first < BIG) & (first % ROWS == rows)
    two = (last >= 0) & (last != first) & (last % ROWS == rows)
    science = jnp.zeros((ROWS, COLS), F32)
    for slot, hit in enumerate((one, two)):
        science = science + lax.dot_general(
            hit.astype(F32).astype(BF16),
            got_ref[:, slot * COLS:(slot + 1) * COLS],
            (((0,), (0,)), ((), ())),
            preferred_element_type=F32,
        )
    science_ref[...] = science

    def step(g, total):
        for b in range(VISITS):
            cut = slice(b * LANES, (b + 1) * LANES)
            lines = science_ref[pl.ds(pl.multiple_of(g * SUB, SUB), SUB), cut]
            for i in range(SUB):
                at = pl.multiple_of((g * SUB + i) * PAD, PAD)
                images = basis_ref[pl.ds(at, PAD), cut].astype(F32)
                total = total + images * lines[i:i + 1, :]
        return total

    total = lax.fori_loop(0, ROWS // SUB, step, jnp.zeros((PAD, LANES), F32))
    moment = jnp.sum(total, axis=1, keepdims=True)
    lane = iota((PAD, LANES), 1)
    gram = jnp.concatenate([gram_ref[...], jnp.zeros((PAD, LANES - PAD), F32)], axis=1)
    part_ref[...] = jnp.where(lane == NB, moment, gram)


def solve_kernel(parts_ref, basis_ref, science_ref, diff_ref, coeff_ref):
    system = parts_ref[0]
    for i in range(1, parts_ref.shape[0]):
        system = system + parts_ref[i]
    sub = iota((PAD, LANES), 0)
    lane = iota((PAD, LANES), 1)
    for p in range(NB):
        column = jnp.broadcast_to(system[:, p:p + 1], (PAD, LANES))
        row = system[p:p + 1, :] / column[p:p + 1, :]
        system = jnp.where(sub == p, row, system - column * row)
    answer = jnp.broadcast_to(system[:, NB:NB + 1], (PAD, LANES))
    coeff_ref[...] = jnp.sum(jnp.where(sub == lane, answer, 0.0), axis=0, keepdims=True)

    def step(g, carry):
        for b in range(VISITS):
            cut = slice(b * LANES, (b + 1) * LANES)
            lines = []
            for i in range(SUB):
                at = pl.multiple_of((g * SUB + i) * PAD, PAD)
                images = basis_ref[pl.ds(at, PAD), cut].astype(F32)
                lines.append(jnp.sum(images * answer, axis=0, keepdims=True))
            here = pl.ds(pl.multiple_of(g * SUB, SUB), SUB)
            diff_ref[here, cut] = science_ref[here, cut] - jnp.concatenate(lines, axis=0)
        return carry

    lax.fori_loop(0, ROWS // SUB, step, 0)


def share(block, axis):
    count = lax.axis_size(axis)
    return lax.all_to_all(
        jnp.broadcast_to(block[None], (count,) + block.shape), axis, 0, 0, tiled=True
    )


def body(template, science_src, target_rows, row_taps, col_taps):
    strip = lax.axis_index(STRIP)
    below = [(i, i + 1) for i in range(STRIPS - 1)]
    above = [(i + 1, i) for i in range(STRIPS - 1)]
    head = lax.ppermute(template[ROWS - HALO:], STRIP, below)
    tail = lax.ppermute(template[:HALO], STRIP, above)

    targets = target_rows.reshape(STRIPS, SRC)
    mine = lax.dynamic_slice_in_dim(targets, strip, 1, 0)
    outgoing = pl.pallas_call(
        send_kernel,
        out_shape=jax.ShapeDtypeStruct((STRIPS, 2 * COLS), BF16),
        in_specs=vmem(2),
        out_specs=vmem(1)[0],
        name="send",
    )(mine, science_src[0])
    incoming = lax.all_to_all(
        outgoing.reshape(STRIPS, 2, COLS), STRIP, 0, 0, tiled=True
    ).reshape(STRIPS, 2 * COLS)

    row_lanes = jnp.pad(row_taps.astype(F32), ((0, PAD - NB), (HALO - REACH, LANES - TAPS - HALO + REACH)))
    left = LANES // 2 - REACH
    col_lanes = jnp.pad(
        col_taps[:, ::-1].astype(F32), ((0, PAD - NB), (left, LANES - TAPS - left))
    )

    framed = jnp.concatenate([head, template, tail], axis=0)
    tiles = share(framed, "visit")
    basis, gram = pl.pallas_call(
        basis_kernel,
        out_shape=(
            jax.ShapeDtypeStruct((ROWS * PAD, COLS), BF16),
            jax.ShapeDtypeStruct((PAD, PAD), F32),
        ),
        in_specs=vmem(3),
        out_specs=tuple(vmem(2)),
        scratch_shapes=[
            pltpu.VMEM((VISITS * FRAME, 2 * LANES), BF16),
            pltpu.VMEM((VISITS, ROWS * PAD, LANES), F32),
        ],
        name="basis",
    )(tiles, row_lanes, col_lanes)
    science, part = pl.pallas_call(
        moment_kernel,
        out_shape=(
            jax.ShapeDtypeStruct((ROWS, COLS), F32),
            jax.ShapeDtypeStruct((PAD, LANES), F32),
        ),
        in_specs=[pl.BlockSpec(memory_space=pltpu.SMEM)] + vmem(4),
        out_specs=tuple(vmem(2)),
        name="moment",
    )(strip.reshape(1), targets, incoming, basis, gram)
    near = jnp.sum(share(part, ("x", "core")), axis=0)
    parts = share(near, "y")
    difference, coeffs = pl.pallas_call(
        solve_kernel,
        out_shape=(
            jax.ShapeDtypeStruct((ROWS, COLS), F32),
            jax.ShapeDtypeStruct((1, LANES), F32),
        ),
        in_specs=vmem(3),
        out_specs=tuple(vmem(2)),
        name="solve",
    )(parts, basis, science)
    return difference[None], coeffs[:, :NB]


def solution(mesh):
    sizes = (VISITS, 8, 4, 2)
    fine = Mesh(mesh.devices.reshape(sizes), ("visit",) + STRIP)
    in_specs = (P(STRIP, "visit"), P("visit", STRIP, None), P("visit", None), P(), P())
    out_specs = (P("visit", STRIP, None), P("visit", None))
    return jax.shard_map(body, mesh=fine, in_specs=in_specs, out_specs=out_specs, check_vma=False)
```

time: 382 us -> 99.3 us (0.26)
  the two profiles are of different devices: /device:TPU:32 before, /device:TPU:2 now
where the time goes in v1:
time: 99.3 us; the launch traced here: 98.6 us
  Pallas kernels  28.4 us (29%)
  starting transfers between devices  27.1 us (27%)
  blocking collectives  26.8 us (27%)
  local copies, waits for them, and re-layouts  7.61 us (8%)
  waiting for transfers between devices  5.28 us (5%)
  other arithmetic  2.72 us (3%)
    all_to_all x2, blocking collectives, share(): lax.all_to_all(jnp.broadcast_to(block[None], (count,) + block.shape), axi...  26.8 us
    pallas_call x1, Pallas kernels, body(): pl.pallas_call(basis_kernel, out_shape=(jax.ShapeDtypeStruct((ROWS * PAD,...  15.3 us
    all_to_all x1, starting transfers between devices, body(): lax.all_to_all(outgoing.reshape(STRIPS, 2, COLS), STRIP, 0, 0, tiled=True)  11.2 us
    all_to_all x1, starting transfers between devices, share(): lax.all_to_all(jnp.broadcast_to(block[None], (count,) + block.shape), axi...  10.3 us
    pallas_call x1, Pallas kernels, body(): pl.pallas_call(solve_kernel, out_shape=(jax.ShapeDtypeStruct((ROWS, COLS)...  7.31 us
    all_to_all x1, waiting for transfers between devices, share(): lax.all_to_all(jnp.broadcast_to(block[None], (count,) + block.shape), axi...  3.98 us
    pallas_call x1, Pallas kernels, body(): pl.pallas_call(moment_kernel, out_shape=(jax.ShapeDtypeStruct((ROWS, COLS...  3.79 us
    ppermute x1, starting transfers between devices, body(): tail = lax.ppermute(template[:HALO], STRIP, above)  3.64 us
  transfers between devices with their start and end apart: 4, of which 2 were waited for; matrix products, arithmetic and copies ran while one was open for 7% of the time, Pallas kernels for 15%

profile of v1, /device:TPU:2, one launch (start us, length us, event | category | flops | bytes accessed | tf_op | source)
XLA Modules:
  0.0 98.6 jit_solution(12199892452115044165)
XLA Ops:
  0.6 0.7 fusion
  1.3 1.9 %collective-permute-start = (bf16[16,128]{1,0:T(8,128)(2,1)S(1)}, bf16[16,128]{1,0:T(8,128)(2,1)S(1)}, u32[]{:S(2)}, u32[]{:S(2)}) collective-permute-start(bf16[16,128]{1,0:T(8,128)(2,1)S(1)} %get-tuple-element.14), channel_id=1, source_target_pairs={{0,1},{1,2},{2,3},{3,4},{4,5},{5,6},{6,7},{7,8},{8,9},{9,10},{10,1... | collective-permute-start | bytes 12296 | tf_op jit(solution)/shard_map/ppermute | solution.py:194
  3.3 3.6 %collective-permute-start.1 = (bf16[16,128]{1,0:T(8,128)(2,1)S(1)}, bf16[16,128]{1,0:T(8,128)(2,1)S(1)}, u32[]{:S(2)}, u32[]{:S(2)}) collective-permute-start(bf16[16,128]{1,0:T(8,128)(2,1)S(1)} %get-tuple-element.15), channel_id=1, source_target_pairs={{1,0},{2,1},{3,2},{4,3},{5,4},{6,5},{7,6},{8,7},{9,8},{10,9},{11,1... | collective-permute-start | bytes 12296 | tf_op jit(solution)/shard_map/ppermute | solution.py:195
  6.9 0.0 collective-permute-done
  6.9 1.3 %collective-permute-done.1 = bf16[16,128]{1,0:T(8,128)(2,1)S(1)} collective-permute-done((bf16[16,128]{1,0:T(8,128)(2,1)S(1)}, bf16[16,128]{1,0:T(8,128)(2,1)S(1)}, u32[]{:S(2)}, u32[]{:S(2)}) %collective-permute-start.1) | collective-permute-done | bytes 4128 | tf_op jit(solution)/shard_map/ppermute | solution.py:195
  8.2 0.7 pad_maximum_fusion
  8.9 0.7 broadcast_in_dim.8
  9.6 10.3 %all-to-all-start.1 = ((bf16[8,64,128]{2,1,0:T(8,128)(2,1)}), bf16[8,64,128]{2,1,0:T(8,128)(2,1)S(1)}, u32[]{:S(2)}, u32[]{:S(2)}) async-start(bf16[8,64,128]{2,1,0:T(8,128)(2,1)} %broadcast_in_dim.8), calls=%async_computation.1 | async-start | bytes 262144 | tf_op jit(solution)/shard_map/all_to_all | solution.py:185
  19.9 0.5 broadcast.10
  20.4 1.3 %reduce.3 = s32[4096]{0:T(1024)S(1)} reduce(s32[1,4096]{1,0:T(1,128)} %param.7, s32[]{:T(128)} %broadcast.10), dimensions={0}, to_apply=%param.7.reduce_sub_computation.3 | reduce | bytes 32772 | tf_op args[2]
  21.7 0.1 reshape.20.targets_ref
  21.8 0.0 copy-start.1
  21.8 0.6 constant_dynamic-slice_fusion.mine_ref
  22.4 2.0 %send.1 = bf16[64,2048]{1,0:T(8,128)(2,1)} custom-call(s32[1,64]{1,0:T(1,128)} %constant_dynamic-slice_fusion.mine_ref, bf16[64,1024]{1,0:T(8,128)(2,1)} %bitcast.8), custom_call_target="tpu_custom_call" | custom-call | tf_op jit(solution)/shard_map/send/pallas_call | solution.py:199
  24.4 1.8 %reshape.21 = bf16[64,2,1024]{2,1,0:T(2,128)(2,1)} reshape(bf16[64,2048]{1,0:T(8,128)(2,1)} %send.1) | data formatting | bytes 524288 | tf_op jit(solution)/shard_map/reshape | solution.py:207
  26.2 4.0 %all-to-all-done.1.tile_ref = bf16[8,64,128]{2,1,0:T(8,128)(2,1)S(1)} async-done(((bf16[8,64,128]{2,1,0:T(8,128)(2,1)}), bf16[8,64,128]{2,1,0:T(8,128)(2,1)S(1)}, u32[]{:S(2)}, u32[]{:S(2)}) %all-to-all-start.1) | async-done | bytes 131104 | tf_op jit(solution)/shard_map/all_to_all | solution.py:185
  30.2 0.0 copy-start
  30.2 11.2 %all-to-all-start = ((bf16[64,2,1024]{2,1,0:T(2,128)(2,1)}), bf16[64,2,1024]{2,1,0:T(2,128)(2,1)S(1)}, u32[]{:S(2)}, u32[]{:S(2)}) async-start(bf16[64,2,1024]{2,1,0:T(2,128)(2,1)} %reshape.21), calls=%async_computation | async-start | bytes 524288 | tf_op jit(solution)/shard_map/all_to_all | solution.py:206
  41.4 0.8 copy.9
  42.2 0.8 copy.10
  43.0 0.1 rev.3
  43.1 0.7 pad_convert_fusion
  43.8 0.0 copy-done
  43.8 15.3 %basis.1 = (bf16[1536,1024]{1,0:T(8,128)(2,1)}, f32[48,48]{1,0:T(8,128)}) custom-call(bf16[8,64,128]{2,1,0:T(8,128)(2,1)} %copy-done, f32[48,128]{1,0:T(8,128)} %get-tuple-element.17.row_ref, f32[48,128]{1,0:T(8,128)} %get-tuple-element.16.col_ref), custom_call_target="tpu_custom_call" | custom-call | tf_op jit(solution)/shard_map/basis/pallas_call | solution.py:218
  59.1 0.0 all-to-all-done
  59.1 0.8 copy.11
  59.8 0.0 copy-done.1
  59.8 3.8 %moment.1 = (f32[32,1024]{1,0:T(8,128)}, f32[48,128]{1,0:T(8,128)}) custom-call(s32[1]{0:T(128)} %bitcast.me_ref, s32[64,64]{1,0:T(8,128)} %copy-done.1, bf16[64,2048]{1,0:T(8,128)(2,1)} %bitcast.6, bf16[1536,1024]{1,0:T(8,128)(2,1)} %get-tuple-element.8.basis_ref, f32[48,48]{1,0:T(8,128)} %get-tuple-element.9.gram_ref), custom_call_target="tpu_custom_call" | custom-call | tf_op jit(solution)/shard_map/moment/pallas_call | solution.py:232
  63.6 0.8 broadcast_in_dim.9
  64.4 9.9 %all_to_all.20 = f32[8,48,128]{2,1,0:T(8,128)S(1)} all-to-all(f32[8,48,128]{2,1,0:T(8,128)S(1)} %broadcast_in_dim.9), channel_id=1, replica_groups=mesh['visit'=8,'y'=8,'x'=4,'core'=2] {'x','core'}, dimensions={0} | all-to-all | bytes 393216 | tf_op jit(solution)/shard_map/all_to_all | solution.py:185
  74.4 16.9 %all_to_all.21.parts_ref = f32[8,48,128]{2,1,0:T(8,128)} all-to-all(f32[8,48,128]{2,1,0:T(8,128)S(1)} %broadcast_in_dim.10), channel_id=1, replica_groups=mesh['visit'=8,'y'=8,'x'=4,'core'=2] {'y'}, dimensions={0} | all-to-all | bytes 393216 | tf_op jit(solution)/shard_map/all_to_all | solution.py:185
  91.3 7.3 %solve.1 = (f32[32,1024]{1,0:T(8,128)}, f32[1,128]{1,0:T(1,128)}) custom-call(f32[8,48,128]{2,1,0:T(8,128)} %all_to_all.21.parts_ref, bf16[1536,1024]{1,0:T(8,128)(2,1)} %get-tuple-element.8.basis_ref, f32[32,1024]{1,0:T(8,128)} %get-tuple-element.11.science_ref), custom_call_target="tpu_custom_call" | custom-call | tf_op jit(solution)/shard_map/solve/pallas_call | solution.py:244
  (2 shorter events, 0.0 us)
Async XLA Ops:
  1.3 5.6 %collective-permute-start = (bf16[16,128]{1,0:T(8,128)(2,1)S(1)}, bf16[16,128]{1,0:T(8,128)(2,1)S(1)}, u32[]{:S(2)}, u32[]{:S(2)}) collective-permute-start(bf16[16,128]{1,0:T(8,128)(2,1)S(1)} %get-tuple-element.14), channel_id=1, source_target_pairs={{0,1},{1,2},{2,3},{3,4},{4,5},{5,6},{6,7},{7,8},{8,9},{9,10},{10,1... | collective-permute-start | bytes 12296 | tf_op jit(solution)/shard_map/ppermute | solution.py:194
  3.3 5.0 %collective-permute-start.1 = (bf16[16,128]{1,0:T(8,128)(2,1)S(1)}, bf16[16,128]{1,0:T(8,128)(2,1)S(1)}, u32[]{:S(2)}, u32[]{:S(2)}) collective-permute-start(bf16[16,128]{1,0:T(8,128)(2,1)S(1)} %get-tuple-element.15), channel_id=1, source_target_pairs={{1,0},{2,1},{3,2},{4,3},{5,4},{6,5},{7,6},{8,7},{9,8},{10,9},{11,1... | collective-permute-start | bytes 12296 | tf_op jit(solution)/shard_map/ppermute | solution.py:195
  9.6 20.6 %all-to-all-start.1 = ((bf16[8,64,128]{2,1,0:T(8,128)(2,1)}), bf16[8,64,128]{2,1,0:T(8,128)(2,1)S(1)}, u32[]{:S(2)}, u32[]{:S(2)}) async-start(bf16[8,64,128]{2,1,0:T(8,128)(2,1)} %broadcast_in_dim.8), calls=%async_computation.1 | async-start | bytes 262144 | tf_op jit(solution)/shard_map/all_to_all | solution.py:185
  21.8 38.0 %copy-start.1 = (s32[64,64]{1,0:T(8,128)}, s32[64,64]{1,0:T(8,128)S(1)}, u32[]{:S(2)}) copy-start(s32[64,64]{1,0:T(8,128)S(1)} %reshape.20.targets_ref) | copy-start | bytes 49156
  30.2 13.6 %copy-start = (bf16[8,64,128]{2,1,0:T(8,128)(2,1)}, bf16[8,64,128]{2,1,0:T(8,128)(2,1)S(1)}, u32[]{:S(2)}) copy-start(bf16[8,64,128]{2,1,0:T(8,128)(2,1)S(1)} %all-to-all-done.1.tile_ref) | copy-start | bytes 393220
  30.2 28.9 %all-to-all-start = ((bf16[64,2,1024]{2,1,0:T(2,128)(2,1)}), bf16[64,2,1024]{2,1,0:T(2,128)(2,1)S(1)}, u32[]{:S(2)}, u32[]{:S(2)}) async-start(bf16[64,2,1024]{2,1,0:T(2,128)(2,1)} %reshape.21), calls=%async_computation | async-start | bytes 524288 | tf_op jit(solution)/shard_map/all_to_all | solution.py:206

commit v2 on v1

v2 whole, which is shorter than its diff:
```python
import jax
import jax.numpy as jnp
from jax import lax
from jax.experimental import pallas as pl
from jax.experimental.pallas import tpu as pltpu
from jax.sharding import Mesh, PartitionSpec as P

STRIPS = 64
VISITS = 8
ROWS = 32
COLS = 1024
LANES = 128
SRC = 64
TAPS = 21
REACH = 10
NB = 45
PAD = 48
HALO = 16
FRAME = ROWS + 2 * HALO
QUAD = 4
QUADS = PAD // QUAD
SUB = 8
TILE = 16
AHEAD = 3
BIG = 1 << 20
F32 = jnp.float32
BF16 = jnp.bfloat16
STRIP = ("y", "x", "core")
MIB = 1 << 20


def vmem(count):
    return [pl.BlockSpec(memory_space=pltpu.VMEM)] * count


def iota(shape, dim):
    return lax.broadcasted_iota(jnp.int32, shape, dim)


def call(kernel, outs, *args, scratch=(), grant=8, far=0):
    return pl.pallas_call(
        kernel,
        out_shape=tuple(jax.ShapeDtypeStruct(*o) for o in outs),
        in_specs=[pl.BlockSpec(memory_space=pltpu.HBM)] * far + vmem(len(args) - far),
        out_specs=tuple(vmem(len(outs))),
        scratch_shapes=list(scratch),
        compiler_params=pltpu.CompilerParams(vmem_limit_bytes=grant * MIB),
    )(*[pltpu.with_memory_space_constraint(arg, pltpu.HBM) for arg in args[:far]], *args[far:])


def my_strip():
    return (lax.axis_index("y") * 4 + lax.axis_index("x")) * 2 + lax.axis_index("core")


def fetch(pairs, sems):
    copies = [pltpu.make_async_copy(far, near, sems.at[i]) for i, (far, near) in enumerate(pairs)]
    for copy in copies:
        copy.start()
    return copies


def prepare_kernel(targets_hbm, src_hbm, out_ref, targets_ref, src_ref, sems):
    copies = fetch([(targets_hbm, targets_ref), (src_hbm, src_ref)], sems)
    for copy in copies:
        copy.wait()
    send(targets_ref, src_ref, out_ref)


def send(targets_ref, src_ref, out_ref):
    strip = my_strip()
    line = jnp.broadcast_to(targets_ref[pl.ds(strip // 2, 1), :], (SUB, LANES))
    line = pltpu.roll(line, (strip % 2) * SRC, 1)
    dest = line[:1, :SRC] // ROWS
    at_dest = dest == iota((STRIPS, SRC), 0)
    order = iota((STRIPS, SRC), 1)
    first = jnp.min(jnp.where(at_dest, order, BIG), axis=1, keepdims=True)
    last = jnp.max(jnp.where(at_dest, order, -1), axis=1, keepdims=True)
    src = src_ref[...]
    one = at_dest & (order == first)
    two = at_dest & (order == last) & (last != first)
    slots = []
    for pick in (one, two):
        rows = jnp.dot(pick.astype(F32).astype(BF16), src, preferred_element_type=F32)
        slots.append(rows.reshape(STRIPS, SUB, LANES))
    out_ref[...] = jnp.concatenate(slots, axis=1).astype(BF16)


def hits(targets_ref, hit_ref):
    strip = my_strip()
    targets = targets_ref[...]
    key = jnp.where(targets // ROWS == strip, (iota(targets.shape, 1) % SRC) * ROWS + targets % ROWS, BIG)
    swapped = jnp.where(key == BIG, -1, key)
    upper = iota(targets.shape, 1) >= SRC
    rows = iota((STRIPS // 2, ROWS), 1)
    for half in range(2):
        mine = upper if half else ~upper
        first = jnp.min(jnp.where(mine, key, BIG), axis=1, keepdims=True)
        last = jnp.max(jnp.where(mine, swapped, -1), axis=1, keepdims=True)
        one = (first < BIG) & (first % ROWS == rows)
        two = (last >= 0) & (last != first) & (last % ROWS == rows)
        hit_ref[half] = one.astype(F32).astype(BF16)
        hit_ref[2 + half] = two.astype(F32).astype(BF16)


def bands(row_ref, col_ref, row_band_ref, col_band_ref, spread_ref):
    spread_ref[...] = jnp.zeros((LANES, LANES), F32)
    spread_ref[HALO - REACH:HALO - REACH + TAPS, :NB] = row_ref[...].astype(F32)
    row_lines = spread_ref[...].T
    spread_ref[...] = jnp.zeros((LANES, LANES), F32)
    top = LANES // 2 + REACH
    col = col_ref[...].astype(F32)
    for t in range(TAPS):
        spread_ref[top - t:top - t + 1, :NB] = col[t:t + 1]
    col_lines = spread_ref[...].T
    above = iota((LANES, LANES), 1) <= iota((LANES, LANES), 0) - (LANES // 2 - REACH)
    blank = jnp.zeros((ROWS, LANES), BF16)
    for k in range(PAD):
        taps = jnp.broadcast_to(col_lines[k:k + 1], (LANES, LANES))
        wheel = pltpu.roll(taps, 0, 1, stride=1, stride_axis=0)
        cut = slice((k % 2) * LANES, (k % 2 + 1) * LANES)
        col_band_ref[k // 2, :LANES, cut] = jnp.where(above, wheel, 0.0).astype(BF16)
        col_band_ref[k // 2, LANES:, cut] = jnp.where(above, 0.0, wheel).astype(BF16)
        taps = jnp.broadcast_to(row_lines[k:k + 1], (ROWS, LANES))
        j = k % QUAD
        band = pltpu.roll(taps, (j % 2) * FRAME, 1, stride=1, stride_axis=0).astype(BF16)
        here = slice(j * ROWS, (j + 1) * ROWS)
        row_band_ref[k // QUAD, here, :LANES] = band if j < 2 else blank
        row_band_ref[k // QUAD, here, LANES:] = blank if j < 2 else band


def basis_kernel(
    row_hbm, col_hbm, own_hbm, above_ref, below_ref,
    basis_ref, gram_ref,
    row_ref, col_ref, own_ref,
    spread_ref, row_band_ref, col_band_ref, win_ref, even_ref, odd_ref, wide_ref, sems,
):
    copies = fetch([(row_hbm, row_ref), (col_hbm, col_ref), (own_hbm, own_ref)], sems)
    copies[0].wait()
    copies[1].wait()
    bands(row_ref, col_ref, row_band_ref, col_band_ref, spread_ref)
    copies[2].wait()
    zero = jnp.zeros((FRAME, LANES // 2), BF16)
    halves = [zero]
    for b in range(VISITS):
        block = jnp.concatenate(
            [above_ref[b, ROWS - HALO:, :], own_ref[b], below_ref[b, :HALO, :]], axis=0
        )
        halves += [block[:, :LANES // 2], block[:, LANES // 2:]]
    halves.append(zero)
    shifted = [jnp.concatenate([halves[2 * i], halves[2 * i + 1]], axis=1) for i in range(VISITS + 1)]
    for b in range(VISITS):
        win_ref[b * FRAME:(b + 1) * FRAME, :LANES] = shifted[b]
        win_ref[b * FRAME:(b + 1) * FRAME, LANES:] = shifted[b + 1]

    def columns(q, smooth_ref):
        for pair in range(QUAD // 2):
            both = jnp.dot(
                win_ref[...], col_band_ref[q * (QUAD // 2) + pair], preferred_element_type=F32
            ).astype(BF16)
            for half in range(2):
                at = (pair * 2 + half) * FRAME
                for b in range(VISITS):
                    smooth_ref[at:at + FRAME, b * LANES:(b + 1) * LANES] = both[
                        b * FRAME:(b + 1) * FRAME, half * LANES:(half + 1) * LANES
                    ]

    def rows(q, smooth_ref):
        done = jnp.dot(row_band_ref[q], smooth_ref[...], preferred_element_type=F32)
        for j in range(QUAD):
            for b in range(VISITS):
                wide_ref[b, pl.ds(q * QUAD + j, ROWS, stride=PAD), :] = done[
                    j * ROWS:(j + 1) * ROWS, b * LANES:(b + 1) * LANES
                ]

    def two(i, carry):
        columns(2 * i + 1, odd_ref)
        rows(2 * i, even_ref)
        columns(2 * i + 2, even_ref)
        rows(2 * i + 1, odd_ref)
        return carry

    columns(0, even_ref)
    lax.fori_loop(0, QUADS // 2 - 1, two, 0)
    columns(QUADS - 1, odd_ref)
    rows(QUADS - 2, even_ref)
    rows(QUADS - 1, odd_ref)

    def gram_step(r, total):
        at = pl.multiple_of(r * PAD, PAD)
        pieces = [wide_ref[b, pl.ds(at, PAD), :].astype(BF16) for b in range(VISITS)]
        for b in range(VISITS):
            basis_ref[b, pl.ds(at, PAD), :] = pieces[b]
        images = jnp.concatenate(pieces, axis=1)
        return total + lax.dot_general(
            images, images, (((1,), (1,)), ((), ())), preferred_element_type=F32
        )

    gram = lax.fori_loop(0, ROWS, gram_step, jnp.zeros((PAD, PAD), F32), unroll=4)
    gram = jnp.concatenate([gram, jnp.zeros((PAD, LANES - PAD), F32)], axis=1)
    lane = iota((TILE, LANES), 1)
    part = gram[:TILE]
    part = jnp.where(lane >= TILE, pltpu.roll(gram[TILE:2 * TILE], TILE, 1), part)
    gram_ref[...] = jnp.where(lane >= 3 * TILE, pltpu.roll(gram[2 * TILE:], 3 * TILE, 1), part)


def moment_kernel(
    targets_hbm, gram_hbm, got_ref, basis_ref, science_ref, part_ref,
    targets_ref, hit_ref, gram_ref, sems,
):
    copies = fetch([(targets_hbm, targets_ref), (gram_hbm, gram_ref)], sems)
    gots = []
    for slot in range(2):
        got = got_ref[:, slot * SUB:(slot + 1) * SUB, :].astype(F32)
        gots.append(got.reshape(STRIPS // 2, 2 * COLS).astype(BF16))
    copies[0].wait()
    hits(targets_ref, hit_ref)
    science = jnp.zeros((ROWS, COLS), F32)
    for slot in range(2):
        got = gots[slot]
        for half in range(2):
            science = science + lax.dot_general(
                hit_ref[slot * 2 + half],
                got[:, half * COLS:(half + 1) * COLS],
                (((0,), (0,)), ((), ())),
                preferred_element_type=F32,
            )
    science_ref[...] = science

    def step(g, total):
        lines = science_ref[pl.ds(pl.multiple_of(g * SUB, SUB), SUB), :]
        for b in range(VISITS):
            for i in range(SUB):
                at = pl.multiple_of((g * SUB + i) * PAD, PAD)
                total = total + basis_ref[b, pl.ds(at, PAD), :].astype(F32) * lines[i:i + 1, b * LANES:(b + 1) * LANES]
        return total

    total = lax.fori_loop(0, ROWS // SUB, step, jnp.zeros((PAD, LANES), F32))
    moment = jnp.sum(total, axis=1, keepdims=True)
    copies[1].wait()
    lane = iota((TILE, LANES), 1)
    part = gram_ref[...]
    for i in range(3):
        part = jnp.where(lane == 6 * TILE + i, moment[i * TILE:(i + 1) * TILE], part)
    for v in range(part_ref.shape[0]):
        part_ref[v] = part


def solve_kernel(parts_ref, basis_ref, science_ref, diff_ref, coeff_ref):
    part = parts_ref[0]
    for i in range(1, parts_ref.shape[0]):
        part = part + parts_ref[i]
    lane = iota((PAD, LANES), 1)
    sub = iota((PAD, LANES), 0)
    lower = jnp.concatenate(
        [part, pltpu.roll(part, LANES - TILE, 1), pltpu.roll(part, LANES - 3 * TILE, 1)], axis=0
    )
    lower = jnp.where(lane // TILE <= sub // TILE, lower, 0.0)
    square = jnp.concatenate([lower, jnp.zeros((LANES - PAD, LANES), F32)], axis=0)
    system = jnp.where(lane // TILE > sub // TILE, square.T[:PAD], lower)
    moment = jnp.concatenate(
        [part[:, 6 * TILE + i:6 * TILE + i + 1] for i in range(3)], axis=0
    )
    system = jnp.where(lane == NB, moment, system)
    ahead = [jnp.broadcast_to(system[:, p:p + 1], (PAD, LANES)) for p in range(AHEAD)]
    for p in range(NB):
        column = ahead.pop(0)
        inverse = 1.0 / column[p:p + 1, :]
        here = sub == p

        def step(values):
            row = values[p:p + 1, :] * inverse
            return jnp.where(here, row, values - column * row)

        ahead = [step(values) for values in ahead]
        system = step(system)
        later = p + AHEAD
        if later <= NB:
            ahead.append(jnp.broadcast_to(system[:, later:later + 1], (PAD, LANES)))
    answer = ahead[0]
    coeff_ref[...] = jnp.sum(jnp.where(sub == lane, answer, 0.0), axis=0, keepdims=True)
    row = iota((SUB, LANES), 0)

    def step(g, carry):
        here = pl.ds(pl.multiple_of(g * SUB, SUB), SUB)
        for b in range(VISITS):
            sums = []
            for i in range(SUB):
                at = pl.multiple_of((g * SUB + i) * PAD, PAD)
                product = basis_ref[b, pl.ds(at, PAD), :].astype(F32) * answer
                total = product[:SUB]
                for n in range(1, PAD // SUB):
                    total = total + product[n * SUB:(n + 1) * SUB]
                sums.append(total)
            span = SUB // 2
            while span:
                keep = (row // span) % 2 == 0
                sums = [
                    jnp.where(keep, sums[i], sums[i + span])
                    + pltpu.roll(jnp.where(keep, sums[i + span], sums[i]), span, 0)
                    for i in range(span)
                ] if span == SUB // 2 else merge(sums, keep, span)
                span //= 2
            cut = slice(b * LANES, (b + 1) * LANES)
            diff_ref[here, cut] = science_ref[here, cut] - sums[0]
        return carry

    lax.fori_loop(0, ROWS // SUB, step, 0)


def merge(sums, keep, span):
    half = len(sums) // 2
    out = []
    for i in range(half):
        a, b = sums[i], sums[i + half]
        low = jnp.where(keep, a, b)
        high = jnp.where(keep, b, a)
        moved = jnp.where(keep, pltpu.roll(high, SUB - span, 0), pltpu.roll(high, span, 0))
        out.append(low + moved)
    return out


def share(block, axis):
    return lax.all_to_all(block, axis, 0, 0, tiled=True)


def body(template, science_src, target_rows, row_taps, col_taps):
    down = [(i, i + 1) for i in range(STRIPS - 1)]
    up = [(i + 1, i) for i in range(STRIPS - 1)]
    copied = jnp.broadcast_to(template[None], (VISITS, ROWS, LANES))
    tiles = share(copied, "visit")
    above = lax.ppermute(tiles, STRIP, down)
    below = lax.ppermute(tiles, STRIP, up)
    targets = target_rows.reshape(STRIPS // 2, 2 * SRC)
    (outgoing,) = call(
        prepare_kernel,
        [((STRIPS, TILE, LANES), BF16)],
        targets,
        science_src[0],
        scratch=[
            pltpu.VMEM(targets.shape, jnp.int32),
            pltpu.VMEM((SRC, COLS), BF16),
            pltpu.SemaphoreType.DMA((2,)),
        ],
        far=2,
    )
    incoming = share(outgoing, STRIP)
    basis, gram = call(
        basis_kernel,
        [((VISITS, ROWS * PAD, LANES), BF16), ((TILE, LANES), F32)],
        row_taps.T,
        col_taps.T,
        tiles,
        above,
        below,
        scratch=[
            pltpu.VMEM((TAPS, NB), BF16),
            pltpu.VMEM((TAPS, NB), BF16),
            pltpu.VMEM((VISITS, ROWS, LANES), BF16),
            pltpu.VMEM((LANES, LANES), F32),
            pltpu.VMEM((QUADS, QUAD * ROWS, 2 * LANES), BF16),
            pltpu.VMEM((PAD // 2, 2 * LANES, 2 * LANES), BF16),
            pltpu.VMEM((VISITS * FRAME, 2 * LANES), BF16),
            pltpu.VMEM((QUAD * FRAME, COLS), BF16),
            pltpu.VMEM((QUAD * FRAME, COLS), BF16),
            pltpu.VMEM((VISITS, ROWS * PAD, LANES), F32),
            pltpu.SemaphoreType.DMA((3,)),
        ],
        grant=24,
        far=3,
    )
    science, part = call(
        moment_kernel,
        [((ROWS, COLS), F32), ((VISITS, TILE, LANES), F32)],
        targets,
        gram,
        incoming,
        basis,
        scratch=[
            pltpu.VMEM(targets.shape, jnp.int32),
            pltpu.VMEM((4, STRIPS // 2, ROWS), BF16),
            pltpu.VMEM((TILE, LANES), F32),
            pltpu.SemaphoreType.DMA((2,)),
        ],
        far=2,
    )
    near = jnp.sum(share(part, ("x", "core")), axis=0)
    parts = share(jnp.broadcast_to(near[None], (VISITS, TILE, LANES)), "y")
    difference, coeffs = call(
        solve_kernel, [((ROWS, COLS), F32), ((1, LANES), F32)], parts, basis, science
    )
    return difference[None], coeffs[:, :NB]


def solution(mesh):
    sizes = (VISITS, 8, 4, 2)
    fine = Mesh(mesh.devices.reshape(sizes), ("visit",) + STRIP)
    in_specs = (P(STRIP, "visit"), P("visit", STRIP, None), P("visit", None), P(), P())
    out_specs = (P("visit", STRIP, None), P("visit", None))
    return jax.shard_map(body, mesh=fine, in_specs=in_specs, out_specs=out_specs, check_vma=False)
```

time: 99.3 us -> 83.2 us (0.84)
  the two profiles are of different devices: /device:TPU:2 before, /device:TPU:1 now
where the time goes in v2:
time: 83.2 us; the launch traced here: 82.5 us
  starting transfers between devices  28.6 us (34%)
  blocking collectives  27.4 us (33%)
  Pallas kernels  17.2 us (21%)
  waiting for transfers between devices  6.6 us (8%)
  local copies, waits for them, and re-layouts  1.94 us (2%)
    all_to_all x2, blocking collectives, share(): return lax.all_to_all(block, axis, 0, 0, tiled=True)  27.4 us
    all_to_all x2, starting transfers between devices, share(): return lax.all_to_all(block, axis, 0, 0, tiled=True)  23.1 us
    pallas_call x4, Pallas kernels, call(): pl.pallas_call(kernel, out_shape=tuple((jax.ShapeDtypeStruct(*o) for o in...  17.2 us
    all_to_all x2, waiting for transfers between devices, share(): return lax.all_to_all(block, axis, 0, 0, tiled=True)  5.1 us
    ppermute x1, starting transfers between devices, body(): above = lax.ppermute(tiles, STRIP, down)  3.2 us
    ppermute x1, starting transfers between devices, body(): below = lax.ppermute(tiles, STRIP, up)  2.36 us
  transfers between devices with their start and end apart: 4, of which 3 were waited for; matrix products, arithmetic and copies ran while one was open for 0% of the time, Pallas kernels for 15%

profile of v2, /device:TPU:1, one launch (start us, length us, event | category | flops | bytes accessed | tf_op | source)
XLA Modules:
  0.0 82.5 jit_solution(12478174130601880102)
XLA Ops:
  0.6 1.3 %broadcast_in_dim.6 = bf16[8,32,128]{2,1,0:T(8,128)(2,1)} broadcast(bf16[32,128]{1,0:T(8,128)(2,1)} %param.5), dimensions={1,2} | broadcast | bytes 73728 | tf_op jit(solution)/shard_map/broadcast_in_dim | solution.py:329
  2.0 10.9 %all-to-all-start = ((bf16[8,32,128]{2,1,0:T(8,128)(2,1)}), bf16[8,32,128]{2,1,0:T(8,128)(2,1)S(1)}, u32[]{:S(2)}, u32[]{:S(2)}) async-start(bf16[8,32,128]{2,1,0:T(8,128)(2,1)} %broadcast_in_dim.6), calls=%async_computation | async-start | bytes 131072 | tf_op jit(solution)/shard_map/all_to_all | solution.py:323
  12.8 2.1 %shard_map.69 = bf16[64,16,128]{2,1,0:T(8,128)(2,1)} custom-call(s32[32,128]{1,0:T(8,128)} %bitcast.7, bf16[64,1024]{1,0:T(8,128)(2,1)} %bitcast.6), custom_call_target="tpu_custom_call" | custom-call | tf_op jit(solution)/shard_map/pallas_call | solution.py:41
  15.0 5.1 %all-to-all-done.own_hbm = bf16[8,32,128]{2,1,0:T(8,128)(2,1)S(1)} async-done(((bf16[8,32,128]{2,1,0:T(8,128)(2,1)}), bf16[8,32,128]{2,1,0:T(8,128)(2,1)S(1)}, u32[]{:S(2)}, u32[]{:S(2)}) %all-to-all-start) | async-done | bytes 65568 | tf_op jit(solution)/shard_map/all_to_all | solution.py:323
  20.1 0.0 copy-start.1
  20.1 12.2 %all-to-all-start.1 = ((bf16[64,16,128]{2,1,0:T(8,128)(2,1)}), bf16[64,16,128]{2,1,0:T(8,128)(2,1)S(1)}, u32[]{:S(2)}, u32[]{:S(2)}) async-start(bf16[64,16,128]{2,1,0:T(8,128)(2,1)} %shard_map.69), calls=%async_computation.1 | async-start | bytes 524288 | tf_op jit(solution)/shard_map/all_to_all | solution.py:323
  32.3 2.4 %collective-permute-start.1 = (bf16[8,32,128]{2,1,0:T(8,128)(2,1)S(1)}, bf16[8,32,128]{2,1,0:T(8,128)(2,1)S(1)}, u32[]{:S(2)}, u32[]{:S(2)}) collective-permute-start(bf16[8,32,128]{2,1,0:T(8,128)(2,1)S(1)} %all-to-all-done.own_hbm), channel_id=1, source_target_pairs={{1,0},{2,1},{3,2},{4,3},{5,4},{6,5},{7,6},{8,7},{9,8},{10,9},{11,1... | collective-permute-start | bytes 196616 | tf_op jit(solution)/shard_map/ppermute | solution.py:332
  34.6 3.2 %collective-permute-start = (bf16[8,32,128]{2,1,0:T(8,128)(2,1)S(1)}, bf16[8,32,128]{2,1,0:T(8,128)(2,1)S(1)}, u32[]{:S(2)}, u32[]{:S(2)}) collective-permute-start(bf16[8,32,128]{2,1,0:T(8,128)(2,1)S(1)} %all-to-all-done.own_hbm), channel_id=1, source_target_pairs={{0,1},{1,2},{2,3},{3,4},{4,5},{5,6},{6,7},{7,8},{8,9},{9,10},{10,1... | collective-permute-start | bytes 196616 | tf_op jit(solution)/shard_map/ppermute | solution.py:331
  37.9 0.8 collective-permute-done.1.below_ref
  38.7 0.7 collective-permute-done.above_ref
  39.4 0.0 copy-done.1
  39.4 10.0 %shard_map.68 = (bf16[8,1536,128]{2,1,0:T(8,128)(2,1)S(1)}, f32[16,128]{1,0:T(8,128)S(1)}) custom-call(bf16[21,45]{1,0:T(8,128)(2,1)} %bitcast.9, bf16[21,45]{1,0:T(8,128)(2,1)} %bitcast.10, bf16[8,32,128]{2,1,0:T(8,128)(2,1)} %copy-done.1, bf16[8,32,128]{2,1,0:T(8,128)(2,1)S(1)} %collective-permute-done.above_ref, ...), custom_call_target="tpu_custom_call" | custom-call | tf_op jit(solution)/shard_map/pallas_call | solution.py:41
  49.4 0.0 copy-start
  49.4 0.6 copy-done
  50.0 0.0 all-to-all-done.1.got_ref
  50.0 1.9 %shard_map.70 = (f32[32,1024]{1,0:T(8,128)S(1)}, f32[8,16,128]{2,1,0:T(8,128)S(1)}) custom-call(s32[32,128]{1,0:T(8,128)} %bitcast.8, f32[16,128]{1,0:T(8,128)} %copy-done, bf16[64,16,128]{2,1,0:T(8,128)(2,1)S(1)} %all-to-all-done.1.got_ref, bf16[8,1536,128]{2,1,0:T(8,128)(2,1)S(1)} %get-tuple-element.9.basis_ref), custom_call_target="tpu_custom_call" | custom-call | tf_op jit(solution)/shard_map/pallas_call | solution.py:41
  51.9 10.9 %all_to_all.20 = f32[8,16,128]{2,1,0:T(8,128)S(1)} all-to-all(f32[8,16,128]{2,1,0:T(8,128)S(1)} %get-tuple-element.10), channel_id=1, replica_groups=mesh['visit'=8,'y'=8,'x'=4,'core'=2] {'x','core'}, dimensions={0} | all-to-all | bytes 131072 | tf_op jit(solution)/shard_map/all_to_all | solution.py:323
  62.9 16.5 %all_to_all.21.parts_ref = f32[8,16,128]{2,1,0:T(8,128)S(1)} all-to-all(f32[8,16,128]{2,1,0:T(8,128)S(1)} %broadcast_in_dim.7), channel_id=1, replica_groups=mesh['visit'=8,'y'=8,'x'=4,'core'=2] {'y'}, dimensions={0} | all-to-all | bytes 131072 | tf_op jit(solution)/shard_map/all_to_all | solution.py:323
  79.4 3.1 %shard_map.71 = (f32[32,1024]{1,0:T(8,128)}, f32[1,128]{1,0:T(1,128)}) custom-call(f32[8,16,128]{2,1,0:T(8,128)S(1)} %all_to_all.21.parts_ref, bf16[8,1536,128]{2,1,0:T(8,128)(2,1)S(1)} %get-tuple-element.9.basis_ref, f32[32,1024]{1,0:T(8,128)S(1)} %get-tuple-element.11.science_ref), custom_call_target="tpu_custom_call" | custom-call | tf_op jit(solution)/shard_map/pallas_call | solution.py:41
  (2 shorter events, 0.0 us)
Async XLA Ops:
  2.0 18.1 %all-to-all-start = ((bf16[8,32,128]{2,1,0:T(8,128)(2,1)}), bf16[8,32,128]{2,1,0:T(8,128)(2,1)S(1)}, u32[]{:S(2)}, u32[]{:S(2)}) async-start(bf16[8,32,128]{2,1,0:T(8,128)(2,1)} %broadcast_in_dim.6), calls=%async_computation | async-start | bytes 131072 | tf_op jit(solution)/shard_map/all_to_all | solution.py:323
  20.1 19.3 %copy-start.1 = (bf16[8,32,128]{2,1,0:T(8,128)(2,1)}, bf16[8,32,128]{2,1,0:T(8,128)(2,1)S(1)}, u32[]{:S(2)}) copy-start(bf16[8,32,128]{2,1,0:T(8,128)(2,1)S(1)} %all-to-all-done.own_hbm) | copy-start | bytes 196612
  20.1 29.9 %all-to-all-start.1 = ((bf16[64,16,128]{2,1,0:T(8,128)(2,1)}), bf16[64,16,128]{2,1,0:T(8,128)(2,1)S(1)}, u32[]{:S(2)}, u32[]{:S(2)}) async-start(bf16[64,16,128]{2,1,0:T(8,128)(2,1)} %shard_map.69), calls=%async_computation.1 | async-start | bytes 524288 | tf_op jit(solution)/shard_map/all_to_all | solution.py:323
  32.3 6.4 %collective-permute-start.1 = (bf16[8,32,128]{2,1,0:T(8,128)(2,1)S(1)}, bf16[8,32,128]{2,1,0:T(8,128)(2,1)S(1)}, u32[]{:S(2)}, u32[]{:S(2)}) collective-permute-start(bf16[8,32,128]{2,1,0:T(8,128)(2,1)S(1)} %all-to-all-done.own_hbm), channel_id=1, source_target_pairs={{1,0},{2,1},{3,2},{4,3},{5,4},{6,5},{7,6},{8,7},{9,8},{10,9},{11,1... | collective-permute-start | bytes 196616 | tf_op jit(solution)/shard_map/ppermute | solution.py:332
  34.6 4.7 %collective-permute-start = (bf16[8,32,128]{2,1,0:T(8,128)(2,1)S(1)}, bf16[8,32,128]{2,1,0:T(8,128)(2,1)S(1)}, u32[]{:S(2)}, u32[]{:S(2)}) collective-permute-start(bf16[8,32,128]{2,1,0:T(8,128)(2,1)S(1)} %all-to-all-done.own_hbm), channel_id=1, source_target_pairs={{0,1},{1,2},{2,3},{3,4},{4,5},{5,6},{6,7},{7,8},{8,9},{9,10},{10,1... | collective-permute-start | bytes 196616 | tf_op jit(solution)/shard_map/ppermute | solution.py:331
  49.4 0.6 copy-start

commit v3 on v2

--- a/solution.py
+++ b/solution.py
@@ -17,8 +17,9 @@
 PAD = 48
 HALO = 16
 FRAME = ROWS + 2 * HALO
-QUAD = 4
-QUADS = PAD // QUAD
+OCT = 8
+OCTS = PAD // OCT
+SPAN = 16
 SUB = 8
 TILE = 16
 AHEAD = 3
@@ -37,12 +38,16 @@
     return lax.broadcasted_iota(jnp.int32, shape, dim)
 
 
-def call(kernel, outs, *args, scratch=(), grant=8, far=0):
+def call(kernel, outs, *args, scratch=(), grant=8, far=0, stay=0):
     return pl.pallas_call(
         kernel,
-        out_shape=tuple(jax.ShapeDtypeStruct(*o) for o in outs),
+        out_shape=tuple(
+            pltpu.HBM(*o) if i < stay else jax.ShapeDtypeStruct(*o) for i, o in enumerate(outs)
+        ),
         in_specs=[pl.BlockSpec(memory_space=pltpu.HBM)] * far + vmem(len(args) - far),
-        out_specs=tuple(vmem(len(outs))),
+        out_specs=tuple(
+            [pl.BlockSpec(memory_space=pltpu.HBM)] * stay + vmem(len(outs) - stay)
+        ),
         scratch_shapes=list(scratch),
         compiler_params=pltpu.CompilerParams(vmem_limit_bytes=grant * MIB),
     )(*[pltpu.with_memory_space_constraint(arg, pltpu.HBM) for arg in args[:far]], *args[far:])
@@ -102,6 +107,14 @@
         hit_ref[2 + half] = two.astype(F32).astype(BF16)
 
 
+def bands_kernel(
+    row_hbm, col_hbm, row_band_ref, col_band_ref, row_ref, col_ref, spread_ref, sems
+):
+    for copy in fetch([(row_hbm, row_ref), (col_hbm, col_ref)], sems):
+        copy.wait()
+    bands(row_ref, col_ref, row_band_ref, col_band_ref, spread_ref)
+
+
 def bands(row_ref, col_ref, row_band_ref, col_band_ref, spread_ref):
     spread_ref[...] = jnp.zeros((LANES, LANES), F32)
     spread_ref[HALO - REACH:HALO - REACH + TAPS, :NB] = row_ref[...].astype(F32)
@@ -113,38 +126,38 @@
         spread_ref[top - t:top - t + 1, :NB] = col[t:t + 1]
     col_lines = spread_ref[...].T
     above = iota((LANES, LANES), 1) <= iota((LANES, LANES), 0) - (LANES // 2 - REACH)
-    blank = jnp.zeros((ROWS, LANES), BF16)
     for k in range(PAD):
         taps = jnp.broadcast_to(col_lines[k:k + 1], (LANES, LANES))
         wheel = pltpu.roll(taps, 0, 1, stride=1, stride_axis=0)
         cut = slice((k % 2) * LANES, (k % 2 + 1) * LANES)
         col_band_ref[k // 2, :LANES, cut] = jnp.where(above, wheel, 0.0).astype(BF16)
         col_band_ref[k // 2, LANES:, cut] = jnp.where(above, 0.0, wheel).astype(BF16)
-        taps = jnp.broadcast_to(row_lines[k:k + 1], (ROWS, LANES))
-        j = k % QUAD
-        band = pltpu.roll(taps, (j % 2) * FRAME, 1, stride=1, stride_axis=0).astype(BF16)
-        here = slice(j * ROWS, (j + 1) * ROWS)
-        row_band_ref[k // QUAD, here, :LANES] = band if j < 2 else blank
-        row_band_ref[k // QUAD, here, LANES:] = blank if j < 2 else band
+    member = iota((2 * OCT, LANES), 0) % OCT
+    for o in range(OCTS):
+        lines = row_lines[o * OCT:(o + 1) * OCT]
+        lines = jnp.where(member[:OCT] % 2 == 1, pltpu.roll(lines, FRAME, 1), lines)
+        for r in range(0, ROWS, 2):
+            moved = [pltpu.roll(lines, r + i, 1) if r + i else lines for i in range(2)]
+            moved = jnp.concatenate(moved, axis=0)
+            for t in range(OCT // 2):
+                row_band_ref[o, r * OCT:(r + 2) * OCT, t * LANES:(t + 1) * LANES] = jnp.where(
+                    member // 2 == t, moved, 0.0
+                ).astype(BF16)
 
 
 def basis_kernel(
-    row_hbm, col_hbm, own_hbm, above_ref, below_ref,
-    basis_ref, gram_ref,
-    row_ref, col_ref, own_ref,
-    spread_ref, row_band_ref, col_band_ref, win_ref, even_ref, odd_ref, wide_ref, sems,
+    own_hbm, far_ref, near_ref, row_band_ref, col_band_ref,
+    basis_ref, own_ref, win_ref, even_ref, odd_ref, wide_ref, sems,
 ):
-    copies = fetch([(row_hbm, row_ref), (col_hbm, col_ref), (own_hbm, own_ref)], sems)
-    copies[0].wait()
-    copies[1].wait()
-    bands(row_ref, col_ref, row_band_ref, col_band_ref, spread_ref)
-    copies[2].wait()
+    for copy in fetch([(own_hbm, own_ref)], sems):
+        copy.wait()
+    first = lax.axis_index("core") == 0
     zero = jnp.zeros((FRAME, LANES // 2), BF16)
     halves = [zero]
     for b in range(VISITS):
-        block = jnp.concatenate(
-            [above_ref[b, ROWS - HALO:, :], own_ref[b], below_ref[b, :HALO, :]], axis=0
-        )
+        above = jnp.where(first, far_ref[b, ROWS - HALO:, :], near_ref[b, ROWS - HALO:, :])
+        below = jnp.where(first, near_ref[b, :HALO, :], far_ref[b, :HALO, :])
+        block = jnp.concatenate([above, own_ref[b], below], axis=0)
         halves += [block[:, :LANES // 2], block[:, LANES // 2:]]
     halves.append(zero)
     shifted = [jnp.concatenate([halves[2 * i], halves[2 * i + 1]], axis=1) for i in range(VISITS + 1)]
@@ -153,9 +166,9 @@
         win_ref[b * FRAME:(b + 1) * FRAME, LANES:] = shifted[b + 1]
 
     def columns(q, smooth_ref):
-        for pair in range(QUAD // 2):
+        for pair in range(OCT // 2):
             both = jnp.dot(
-                win_ref[...], col_band_ref[q * (QUAD // 2) + pair], preferred_element_type=F32
+                win_ref[...], col_band_ref[q * (OCT // 2) + pair], preferred_element_type=F32
             ).astype(BF16)
             for half in range(2):
                 at = (pair * 2 + half) * FRAME
@@ -166,10 +179,11 @@
 
     def rows(q, smooth_ref):
         done = jnp.dot(row_band_ref[q], smooth_ref[...], preferred_element_type=F32)
-        for j in range(QUAD):
+        for r in range(ROWS):
+            at = pl.multiple_of(r * PAD + q * OCT, OCT)
             for b in range(VISITS):
-                wide_ref[b, pl.ds(q * QUAD + j, ROWS, stride=PAD), :] = done[
-                    j * ROWS:(j + 1) * ROWS, b * LANES:(b + 1) * LANES
+                wide_ref[b, pl.ds(at, OCT), :] = done[
+                    r * OCT:(r + 1) * OCT, b * LANES:(b + 1) * LANES
                 ]
 
     def two(i, carry):
@@ -180,34 +194,40 @@
         return carry
 
     columns(0, even_ref)
-    lax.fori_loop(0, QUADS // 2 - 1, two, 0)
-    columns(QUADS - 1, odd_ref)
-    rows(QUADS - 2, even_ref)
-    rows(QUADS - 1, odd_ref)
-
-    def gram_step(r, total):
-        at = pl.multiple_of(r * PAD, PAD)
-        pieces = [wide_ref[b, pl.ds(at, PAD), :].astype(BF16) for b in range(VISITS)]
-        for b in range(VISITS):
-            basis_ref[b, pl.ds(at, PAD), :] = pieces[b]
+    lax.fori_loop(0, OCTS // 2 - 1, two, 0)
+    columns(OCTS - 1, odd_ref)
+    rows(OCTS - 2, even_ref)
+    rows(OCTS - 1, odd_ref)
+
+    def gram_step(g, total):
+        pieces = []
+        for i in range(SPAN):
+            at = pl.multiple_of((g * SPAN + i) * PAD, PAD)
+            for b in range(VISITS):
+                piece = wide_ref[b, pl.ds(at, PAD), :].astype(BF16)
+                basis_ref[b, pl.ds(at, PAD), :] = piece
+                pieces.append(piece)
         images = jnp.concatenate(pieces, axis=1)
         return total + lax.dot_general(
             images, images, (((1,), (1,)), ((), ())), preferred_element_type=F32
         )
 
-    gram = lax.fori_loop(0, ROWS, gram_step, jnp.zeros((PAD, PAD), F32), unroll=4)
+    gram = lax.fori_loop(0, ROWS // SPAN, gram_step, jnp.zeros((PAD, PAD), F32))
     gram = jnp.concatenate([gram, jnp.zeros((PAD, LANES - PAD), F32)], axis=1)
     lane = iota((TILE, LANES), 1)
     part = gram[:TILE]
     part = jnp.where(lane >= TILE, pltpu.roll(gram[TILE:2 * TILE], TILE, 1), part)
-    gram_ref[...] = jnp.where(lane >= 3 * TILE, pltpu.roll(gram[2 * TILE:], 3 * TILE, 1), part)
+    rest = jnp.where(lane >= 3 * TILE, pltpu.roll(gram[2 * TILE:], 3 * TILE, 1), part)
+    for i in range(3):
+        piece = rest.astype(BF16)
+        basis_ref[0, ROWS * PAD + i * TILE:ROWS * PAD + (i + 1) * TILE, :] = piece
+        rest = rest - piece.astype(F32)
 
 
 def moment_kernel(
-    targets_hbm, gram_hbm, got_ref, basis_ref, science_ref, part_ref,
-    targets_ref, hit_ref, gram_ref, sems,
+    targets_hbm, got_ref, basis_ref, science_hbm, part_ref, science_ref, targets_ref, hit_ref, sems
 ):
-    copies = fetch([(targets_hbm, targets_ref), (gram_hbm, gram_ref)], sems)
+    copies = fetch([(targets_hbm, targets_ref)], sems)
     gots = []
     for slot in range(2):
         got = got_ref[:, slot * SUB:(slot + 1) * SUB, :].astype(F32)
@@ -225,6 +245,8 @@
                 preferred_element_type=F32,
             )
     science_ref[...] = science
+    keep = pltpu.make_async_copy(science_ref, science_hbm, sems.at[1])
+    keep.start()
 
     def step(g, total):
         lines = science_ref[pl.ds(pl.multiple_of(g * SUB, SUB), SUB), :]
@@ -236,16 +258,20 @@
 
     total = lax.fori_loop(0, ROWS // SUB, step, jnp.zeros((PAD, LANES), F32))
     moment = jnp.sum(total, axis=1, keepdims=True)
-    copies[1].wait()
     lane = iota((TILE, LANES), 1)
-    part = gram_ref[...]
+    part = jnp.zeros((TILE, LANES), F32)
+    for i in (2, 1, 0):
+        at = ROWS * PAD + i * TILE
+        part = part + basis_ref[0, at:at + TILE, :].astype(F32)
     for i in range(3):
         part = jnp.where(lane == 6 * TILE + i, moment[i * TILE:(i + 1) * TILE], part)
     for v in range(part_ref.shape[0]):
         part_ref[v] = part
-
-
-def solve_kernel(parts_ref, basis_ref, science_ref, diff_ref, coeff_ref):
+    keep.wait()
+
+
+def solve_kernel(science_hbm, parts_ref, basis_ref, diff_ref, coeff_ref, science_ref, sems):
+    copies = fetch([(science_hbm, science_ref)], sems)
     part = parts_ref[0]
     for i in range(1, parts_ref.shape[0]):
         part = part + parts_ref[i]
@@ -279,6 +305,7 @@
     answer = ahead[0]
     coeff_ref[...] = jnp.sum(jnp.where(sub == lane, answer, 0.0), axis=0, keepdims=True)
     row = iota((SUB, LANES), 0)
+    copies[0].wait()
 
     def step(g, carry):
         here = pl.ds(pl.multiple_of(g * SUB, SUB), SUB)
@@ -324,12 +351,10 @@
 
 
 def body(template, science_src, target_rows, row_taps, col_taps):
-    down = [(i, i + 1) for i in range(STRIPS - 1)]
-    up = [(i + 1, i) for i in range(STRIPS - 1)]
+    inner = [(i, i ^ 1) for i in range(STRIPS)]
+    outer = [(i, i + 1 if i % 2 else i - 1) for i in range(1, STRIPS - 1)]
     copied = jnp.broadcast_to(template[None], (VISITS, ROWS, LANES))
     tiles = share(copied, "visit")
-    above = lax.ppermute(tiles, STRIP, down)
-    below = lax.ppermute(tiles, STRIP, up)
     targets = target_rows.reshape(STRIPS // 2, 2 * SRC)
     (outgoing,) = call(
         prepare_kernel,
@@ -344,49 +369,65 @@
         far=2,
     )
     incoming = share(outgoing, STRIP)
-    basis, gram = call(
-        basis_kernel,
-        [((VISITS, ROWS * PAD, LANES), BF16), ((TILE, LANES), F32)],
+    far_tiles = lax.ppermute(tiles, STRIP, outer)
+    near_tiles = lax.ppermute(tiles, STRIP, inner)
+    row_bands, col_bands = call(
+        bands_kernel,
+        [((OCTS, OCT * ROWS, OCT * FRAME), BF16), ((PAD // 2, 2 * LANES, 2 * LANES), BF16)],
         row_taps.T,
         col_taps.T,
-        tiles,
-        above,
-        below,
         scratch=[
             pltpu.VMEM((TAPS, NB), BF16),
             pltpu.VMEM((TAPS, NB), BF16),
+            pltpu.VMEM((LANES, LANES), F32),
+            pltpu.SemaphoreType.DMA((2,)),
+        ],
+        far=2,
+    )
+    (basis,) = call(
+        basis_kernel,
+        [((VISITS, ROWS * PAD + 3 * TILE, LANES), BF16)],
+        tiles,
+        far_tiles,
+        near_tiles,
+        row_bands,
+        col_bands,
+        scratch=[
             pltpu.VMEM((VISITS, ROWS, LANES), BF16),
-            pltpu.VMEM((LANES, LANES), F32),
-            pltpu.VMEM((QUADS, QUAD * ROWS, 2 * LANES), BF16),
-            pltpu.VMEM((PAD // 2, 2 * LANES, 2 * LANES), BF16),
             pltpu.VMEM((VISITS * FRAME, 2 * LANES), BF16),
-            pltpu.VMEM((QUAD * FRAME, COLS), BF16),
-            pltpu.VMEM((QUAD * FRAME, COLS), BF16),
+            pltpu.VMEM((OCT * FRAME, COLS), BF16),
+            pltpu.VMEM((OCT * FRAME, COLS), BF16),
             pltpu.VMEM((VISITS, ROWS * PAD, LANES), F32),
-            pltpu.SemaphoreType.DMA((3,)),
+            pltpu.SemaphoreType.DMA((1,)),
         ],
         grant=24,
-        far=3,
+        far=1,
     )
     science, part = call(
         moment_kernel,
         [((ROWS, COLS), F32), ((VISITS, TILE, LANES), F32)],
         targets,
-        gram,
         incoming,
         basis,
         scratch=[
+            pltpu.VMEM((ROWS, COLS), F32),
             pltpu.VMEM(targets.shape, jnp.int32),
             pltpu.VMEM((4, STRIPS // 2, ROWS), BF16),
-            pltpu.VMEM((TILE, LANES), F32),
             pltpu.SemaphoreType.DMA((2,)),
         ],
-        far=2,
+        far=1,
+        stay=1,
     )
     near = jnp.sum(share(part, ("x", "core")), axis=0)
     parts = share(jnp.broadcast_to(near[None], (VISITS, TILE, LANES)), "y")
     difference, coeffs = call(
-        solve_kernel, [((ROWS, COLS), F32), ((1, LANES), F32)], parts, basis, science
+        solve_kernel,
+        [((ROWS, COLS), F32), ((1, LANES), F32)],
+        science,
+        parts,
+        basis,
+        scratch=[pltpu.VMEM((ROWS, COLS), F32), pltpu.SemaphoreType.DMA((1,))],
+        far=1,
     )
     return difference[None], coeffs[:, :NB]
 

time: 83.2 us -> 75.7 us (0.910)
  blocking collectives: 27.4 us -> 23.8 us
  Pallas kernels: 17.2 us -> 15.4 us
  waiting for transfers between devices: 6.6 us -> 5.1 us
    all_to_all x2, blocking collectives: 27.4 us -> 23.8 us  [share(): return lax.all_to_all(block, axis, 0, 0, tiled=True)]
    pallas_call x4 -> x5, Pallas kernels: 17.2 us -> 15.4 us  [call(): pl.pallas_call(kernel, out_shape=tuple((pltpu.HBM(*o) if i < stay else ja...]
    ppermute x2, waiting for transfers between devices: 1.49 us -> 0.01 us  [the longest x1 0.01 us: body(): far_tiles = lax.ppermute(tiles, STRIP, outer)]
  transfers between devices with their start and end apart: 4 -> 4, of which waited for: 3 -> 1; matrix products, arithmetic and copies ran while one was open for 0% -> 0% of each run, Pallas kernels for 15% -> 14%
where the time goes in v3:
time: 75.7 us; the launch traced here: 75 us
  starting transfers between devices  28.5 us (38%)
  blocking collectives  23.8 us (31%)
  Pallas kernels  15.4 us (20%)
  waiting for transfers between devices  5.1 us (7%)
  local copies, waits for them, and re-layouts  1.35 us (2%)
    all_to_all x2, blocking collectives, share(): return lax.all_to_all(block, axis, 0, 0, tiled=True)  23.8 us
    all_to_all x2, starting transfers between devices, share(): return lax.all_to_all(block, axis, 0, 0, tiled=True)  23.1 us
    pallas_call x5, Pallas kernels, call(): pl.pallas_call(kernel, out_shape=tuple((pltpu.HBM(*o) if i < stay else ja...  15.4 us
    all_to_all x2, waiting for transfers between devices, share(): return lax.all_to_all(block, axis, 0, 0, tiled=True)  5.1 us
    ppermute x1, starting transfers between devices, body(): far_tiles = lax.ppermute(tiles, STRIP, outer)  3.54 us
    ppermute x1, starting transfers between devices, body(): near_tiles = lax.ppermute(tiles, STRIP, inner)  1.92 us
  transfers between devices with their start and end apart: 4, of which 1 were waited for; matrix products, arithmetic and copies ran while one was open for 0% of the time, Pallas kernels for 14%

profile of v3, /device:TPU:1, one launch (start us, length us, event | category | flops | bytes accessed | tf_op | source)
XLA Modules:
  0.0 75.0 jit_solution(17196962568129990220)
XLA Ops:
  0.6 1.3 %broadcast_in_dim.6 = bf16[8,32,128]{2,1,0:T(8,128)(2,1)} broadcast(bf16[32,128]{1,0:T(8,128)(2,1)} %param.5), dimensions={1,2} | broadcast | bytes 73728 | tf_op jit(solution)/shard_map/broadcast_in_dim | solution.py:356
  2.0 10.9 %all-to-all-start.1 = ((bf16[8,32,128]{2,1,0:T(8,128)(2,1)}), bf16[8,32,128]{2,1,0:T(8,128)(2,1)S(1)}, u32[]{:S(2)}, u32[]{:S(2)}) async-start(bf16[8,32,128]{2,1,0:T(8,128)(2,1)} %broadcast_in_dim.6), calls=%async_computation.1 | async-start | bytes 131072 | tf_op jit(solution)/shard_map/all_to_all | solution.py:350
  12.8 2.1 %shard_map.68 = bf16[64,16,128]{2,1,0:T(8,128)(2,1)} custom-call(s32[32,128]{1,0:T(8,128)} %bitcast.7, bf16[64,1024]{1,0:T(8,128)(2,1)} %bitcast.6), custom_call_target="tpu_custom_call" | custom-call | tf_op jit(solution)/shard_map/pallas_call | solution.py:42
  15.0 5.1 %all-to-all-done.1.own_hbm = bf16[8,32,128]{2,1,0:T(8,128)(2,1)S(1)} async-done(((bf16[8,32,128]{2,1,0:T(8,128)(2,1)}), bf16[8,32,128]{2,1,0:T(8,128)(2,1)S(1)}, u32[]{:S(2)}, u32[]{:S(2)}) %all-to-all-start.1) | async-done | bytes 65568 | tf_op jit(solution)/shard_map/all_to_all | solution.py:350
  20.1 0.0 copy-start
  20.1 12.2 %all-to-all-start = ((bf16[64,16,128]{2,1,0:T(8,128)(2,1)}), bf16[64,16,128]{2,1,0:T(8,128)(2,1)S(1)}, u32[]{:S(2)}, u32[]{:S(2)}) async-start(bf16[64,16,128]{2,1,0:T(8,128)(2,1)} %shard_map.68), calls=%async_computation | async-start | bytes 524288 | tf_op jit(solution)/shard_map/all_to_all | solution.py:350
  32.3 3.5 %collective-permute-start = (bf16[8,32,128]{2,1,0:T(8,128)(2,1)S(1)}, bf16[8,32,128]{2,1,0:T(8,128)(2,1)S(1)}, u32[]{:S(2)}, u32[]{:S(2)}) collective-permute-start(bf16[8,32,128]{2,1,0:T(8,128)(2,1)S(1)} %all-to-all-done.1.own_hbm), channel_id=1, source_target_pairs={{1,2},{2,1},{3,4},{4,3},{5,6},{6,5},{7,8},{8,7},{9,10},{10,9},{11,... | collective-permute-start | bytes 196616 | tf_op jit(solution)/shard_map/ppermute | solution.py:372
  35.8 1.9 %collective-permute-start.1 = (bf16[8,32,128]{2,1,0:T(8,128)(2,1)S(1)}, bf16[8,32,128]{2,1,0:T(8,128)(2,1)S(1)}, u32[]{:S(2)}, u32[]{:S(2)}) collective-permute-start(bf16[8,32,128]{2,1,0:T(8,128)(2,1)S(1)} %all-to-all-done.1.own_hbm), channel_id=1, source_target_pairs={{0,1},{1,0},{2,3},{3,2},{4,5},{5,4},{6,7},{7,6},{8,9},{9,8},{10,11... | collective-permute-start | bytes 196616 | tf_op jit(solution)/shard_map/ppermute | solution.py:373
  37.8 1.8 %shard_map.69 = (bf16[6,256,512]{2,1,0:T(8,128)(2,1)S(1)}, bf16[24,256,256]{2,1,0:T(8,128)(2,1)S(1)}) custom-call(bf16[21,45]{1,0:T(8,128)(2,1)} %bitcast.9, bf16[21,45]{1,0:T(8,128)(2,1)} %bitcast.10), custom_call_target="tpu_custom_call" | custom-call | tf_op jit(solution)/shard_map/pallas_call | solution.py:42
  39.6 0.0 collective-permute-done.far_ref
  39.6 0.0 collective-permute-done.1.near_ref
  39.6 0.0 copy-done
  39.6 6.5 %shard_map.70.basis_ref = bf16[8,1584,128]{2,1,0:T(8,128)(2,1)S(1)} custom-call(bf16[8,32,128]{2,1,0:T(8,128)(2,1)} %copy-done, bf16[8,32,128]{2,1,0:T(8,128)(2,1)S(1)} %collective-permute-done.far_ref, bf16[8,32,128]{2,1,0:T(8,128)(2,1)S(1)} %collective-permute-done.1.near_ref, bf16[6,256,512]{2,1,0:T(8,128)(2,1)S(1)} %get-tuple-element.8.row_band_ref, ...), custom_call_target="tpu_custom_call" | custom-call | tf_op jit(solution)/shard_map/pallas_call | solution.py:42
  46.0 0.0 all-to-all-done.got_ref
  46.1 1.9 %shard_map.71 = (f32[32,1024]{1,0:T(8,128)}, f32[8,16,128]{2,1,0:T(8,128)S(1)}) custom-call(s32[32,128]{1,0:T(8,128)} %bitcast.8, bf16[64,16,128]{2,1,0:T(8,128)(2,1)S(1)} %all-to-all-done.got_ref, bf16[8,1584,128]{2,1,0:T(8,128)(2,1)S(1)} %shard_map.70.basis_ref), custom_call_target="tpu_custom_call" | custom-call | tf_op jit(solution)/shard_map/pallas_call | solution.py:42
  48.0 10.2 %all_to_all.20 = f32[8,16,128]{2,1,0:T(8,128)S(1)} all-to-all(f32[8,16,128]{2,1,0:T(8,128)S(1)} %get-tuple-element.11), channel_id=1, replica_groups=mesh['visit'=8,'y'=8,'x'=4,'core'=2] {'x','core'}, dimensions={0} | all-to-all | bytes 131072 | tf_op jit(solution)/shard_map/all_to_all | solution.py:350
  58.2 13.6 %all_to_all.21.parts_ref = f32[8,16,128]{2,1,0:T(8,128)S(1)} all-to-all(f32[8,16,128]{2,1,0:T(8,128)S(1)} %broadcast_in_dim.7), channel_id=1, replica_groups=mesh['visit'=8,'y'=8,'x'=4,'core'=2] {'y'}, dimensions={0} | all-to-all | bytes 131072 | tf_op jit(solution)/shard_map/all_to_all | solution.py:350
  71.8 3.2 %shard_map.72 = (f32[32,1024]{1,0:T(8,128)}, f32[1,128]{1,0:T(1,128)}) custom-call(f32[32,1024]{1,0:T(8,128)} %get-tuple-element.10.science_hbm, f32[8,16,128]{2,1,0:T(8,128)S(1)} %all_to_all.21.parts_ref, bf16[8,1584,128]{2,1,0:T(8,128)(2,1)S(1)} %shard_map.70.basis_ref), custom_call_target="tpu_custom_call" | custom-call | tf_op jit(solution)/shard_map/pallas_call | solution.py:42
  (2 shorter events, 0.0 us)
Async XLA Ops:
  2.0 18.1 %all-to-all-start.1 = ((bf16[8,32,128]{2,1,0:T(8,128)(2,1)}), bf16[8,32,128]{2,1,0:T(8,128)(2,1)S(1)}, u32[]{:S(2)}, u32[]{:S(2)}) async-start(bf16[8,32,128]{2,1,0:T(8,128)(2,1)} %broadcast_in_dim.6), calls=%async_computation.1 | async-start | bytes 131072 | tf_op jit(solution)/shard_map/all_to_all | solution.py:350
  20.1 19.5 %copy-start = (bf16[8,32,128]{2,1,0:T(8,128)(2,1)}, bf16[8,32,128]{2,1,0:T(8,128)(2,1)S(1)}, u32[]{:S(2)}) copy-start(bf16[8,32,128]{2,1,0:T(8,128)(2,1)S(1)} %all-to-all-done.1.own_hbm) | copy-start | bytes 196612
  20.1 26.0 %all-to-all-start = ((bf16[64,16,128]{2,1,0:T(8,128)(2,1)}), bf16[64,16,128]{2,1,0:T(8,128)(2,1)S(1)}, u32[]{:S(2)}, u32[]{:S(2)}) async-start(bf16[64,16,128]{2,1,0:T(8,128)(2,1)} %shard_map.68), calls=%async_computation | async-start | bytes 524288 | tf_op jit(solution)/shard_map/all_to_all | solution.py:350
  32.3 7.3 %collective-permute-start = (bf16[8,32,128]{2,1,0:T(8,128)(2,1)S(1)}, bf16[8,32,128]{2,1,0:T(8,128)(2,1)S(1)}, u32[]{:S(2)}, u32[]{:S(2)}) collective-permute-start(bf16[8,32,128]{2,1,0:T(8,128)(2,1)S(1)} %all-to-all-done.1.own_hbm), channel_id=1, source_target_pairs={{1,2},{2,1},{3,4},{4,3},{5,6},{6,5},{7,8},{8,7},{9,10},{10,9},{11,... | collective-permute-start | bytes 196616 | tf_op jit(solution)/shard_map/ppermute | solution.py:372
  35.8 3.7 %collective-permute-start.1 = (bf16[8,32,128]{2,1,0:T(8,128)(2,1)S(1)}, bf16[8,32,128]{2,1,0:T(8,128)(2,1)S(1)}, u32[]{:S(2)}, u32[]{:S(2)}) collective-permute-start(bf16[8,32,128]{2,1,0:T(8,128)(2,1)S(1)} %all-to-all-done.1.own_hbm), channel_id=1, source_target_pairs={{0,1},{1,0},{2,3},{3,2},{4,5},{5,4},{6,7},{7,6},{8,9},{9,8},{10,11... | collective-permute-start | bytes 196616 | tf_op jit(solution)/shard_map/ppermute | solution.py:373

commit v4 on v3

--- a/solution.py
+++ b/solution.py
@@ -22,7 +22,7 @@
 SPAN = 16
 SUB = 8
 TILE = 16
-AHEAD = 3
+AHEAD = 8
 BIG = 1 << 20
 F32 = jnp.float32
 BF16 = jnp.bfloat16
@@ -103,15 +103,19 @@
         last = jnp.max(jnp.where(mine, swapped, -1), axis=1, keepdims=True)
         one = (first < BIG) & (first % ROWS == rows)
         two = (last >= 0) & (last != first) & (last % ROWS == rows)
-        hit_ref[half] = one.astype(F32).astype(BF16)
-        hit_ref[2 + half] = two.astype(F32).astype(BF16)
+        blank = jnp.zeros((STRIPS // 2, LANES - ROWS), F32)
+        for slot, pick in enumerate((one, two)):
+            pick = jnp.concatenate([pick.astype(F32), blank], axis=1)
+            hit_ref[slot * 2 + half] = pick.astype(BF16)
 
 
 def bands_kernel(
-    row_hbm, col_hbm, row_band_ref, col_band_ref, row_ref, col_ref, spread_ref, sems
+    row_hbm, col_hbm, targets_hbm, row_band_ref, col_band_ref, hit_ref,
+    row_ref, col_ref, targets_ref, spread_ref, sems,
 ):
-    for copy in fetch([(row_hbm, row_ref), (col_hbm, col_ref)], sems):
+    for copy in fetch([(row_hbm, row_ref), (col_hbm, col_ref), (targets_hbm, targets_ref)], sems):
         copy.wait()
+    hits(targets_ref, hit_ref)
     bands(row_ref, col_ref, row_band_ref, col_band_ref, spread_ref)
 
 
@@ -146,11 +150,13 @@
 
 
 def basis_kernel(
-    own_hbm, far_ref, near_ref, row_band_ref, col_band_ref,
+    own_hbm, far_ref, near_ref, row_band_ref, col_band_ref, hit_ref,
     basis_ref, own_ref, win_ref, even_ref, odd_ref, wide_ref, sems,
 ):
-    for copy in fetch([(own_hbm, own_ref)], sems):
-        copy.wait()
+    copies = fetch([(own_hbm, own_ref)], sems)
+    for i in range(4):
+        basis_ref[1 + i, ROWS * PAD:ROWS * PAD + STRIPS // 2, :] = hit_ref[i]
+    copies[0].wait()
     first = lax.axis_index("core") == 0
     zero = jnp.zeros((FRAME, LANES // 2), BF16)
     halves = [zero]
@@ -225,27 +231,24 @@
 
 
 def moment_kernel(
-    targets_hbm, got_ref, basis_ref, science_hbm, part_ref, science_ref, targets_ref, hit_ref, sems
+    got_ref, basis_ref, science_hbm, part_ref, science_ref, sem
 ):
-    copies = fetch([(targets_hbm, targets_ref)], sems)
     gots = []
     for slot in range(2):
         got = got_ref[:, slot * SUB:(slot + 1) * SUB, :].astype(F32)
         gots.append(got.reshape(STRIPS // 2, 2 * COLS).astype(BF16))
-    copies[0].wait()
-    hits(targets_ref, hit_ref)
     science = jnp.zeros((ROWS, COLS), F32)
     for slot in range(2):
         got = gots[slot]
         for half in range(2):
             science = science + lax.dot_general(
-                hit_ref[slot * 2 + half],
+                basis_ref[1 + slot * 2 + half, ROWS * PAD:ROWS * PAD + STRIPS // 2, :ROWS],
                 got[:, half * COLS:(half + 1) * COLS],
                 (((0,), (0,)), ((), ())),
                 preferred_element_type=F32,
             )
     science_ref[...] = science
-    keep = pltpu.make_async_copy(science_ref, science_hbm, sems.at[1])
+    keep = pltpu.make_async_copy(science_ref, science_hbm, sem)
     keep.start()
 
     def step(g, total):
@@ -371,18 +374,20 @@
     incoming = share(outgoing, STRIP)
     far_tiles = lax.ppermute(tiles, STRIP, outer)
     near_tiles = lax.ppermute(tiles, STRIP, inner)
-    row_bands, col_bands = call(
+    row_bands, col_bands, hit = call(
         bands_kernel,
-        [((OCTS, OCT * ROWS, OCT * FRAME), BF16), ((PAD // 2, 2 * LANES, 2 * LANES), BF16)],
+        [((OCTS, OCT * ROWS, OCT * FRAME), BF16), ((PAD // 2, 2 * LANES, 2 * LANES), BF16), ((4, STRIPS // 2, LANES), BF16)],
         row_taps.T,
         col_taps.T,
+        targets,
         scratch=[
             pltpu.VMEM((TAPS, NB), BF16),
             pltpu.VMEM((TAPS, NB), BF16),
+            pltpu.VMEM(targets.shape, jnp.int32),
             pltpu.VMEM((LANES, LANES), F32),
-            pltpu.SemaphoreType.DMA((2,)),
+            pltpu.SemaphoreType.DMA((3,)),
         ],
-        far=2,
+        far=3,
     )
     (basis,) = call(
         basis_kernel,
@@ -392,6 +397,7 @@
         near_tiles,
         row_bands,
         col_bands,
+        hit,
         scratch=[
             pltpu.VMEM((VISITS, ROWS, LANES), BF16),
             pltpu.VMEM((VISITS * FRAME, 2 * LANES), BF16),
@@ -406,16 +412,9 @@
     science, part = call(
         moment_kernel,
         [((ROWS, COLS), F32), ((VISITS, TILE, LANES), F32)],
-        targets,
         incoming,
         basis,
-        scratch=[
-            pltpu.VMEM((ROWS, COLS), F32),
-            pltpu.VMEM(targets.shape, jnp.int32),
-            pltpu.VMEM((4, STRIPS // 2, ROWS), BF16),
-            pltpu.SemaphoreType.DMA((2,)),
-        ],
-        far=1,
+        scratch=[pltpu.VMEM((ROWS, COLS), F32), pltpu.SemaphoreType.DMA],
         stay=1,
     )
     near = jnp.sum(share(part, ("x", "core")), axis=0)

time: 75.7 us -> 74 us (0.978)
  Pallas kernels: 15.4 us -> 14 us
    pallas_call x5, Pallas kernels: 15.4 us -> 14 us  [call(): pl.pallas_call(kernel, out_shape=tuple((pltpu.HBM(*o) if i < stay else ja...]
where the time goes in v4:
time: 74 us; the launch traced here: 73.3 us
  starting transfers between devices  28.5 us (39%)
  blocking collectives  23.6 us (32%)
  Pallas kernels  14 us (19%)
  waiting for transfers between devices  5.1 us (7%)
  local copies, waits for them, and re-layouts  1.35 us (2%)
    all_to_all x2, blocking collectives, share(): return lax.all_to_all(block, axis, 0, 0, tiled=True)  23.6 us
    all_to_all x2, starting transfers between devices, share(): return lax.all_to_all(block, axis, 0, 0, tiled=True)  23.1 us
    pallas_call x5, Pallas kernels, call(): pl.pallas_call(kernel, out_shape=tuple((pltpu.HBM(*o) if i < stay else ja...  14 us
    all_to_all x2, waiting for transfers between devices, share(): return lax.all_to_all(block, axis, 0, 0, tiled=True)  5.1 us
    ppermute x1, starting transfers between devices, body(): far_tiles = lax.ppermute(tiles, STRIP, outer)  3.54 us
    ppermute x1, starting transfers between devices, body(): near_tiles = lax.ppermute(tiles, STRIP, inner)  1.92 us
  transfers between devices with their start and end apart: 4, of which 1 were waited for; matrix products, arithmetic and copies ran while one was open for 0% of the time, Pallas kernels for 14%

profile of v4, /device:TPU:1, one launch (start us, length us, event | category | flops | bytes accessed | tf_op | source)
XLA Modules:
  0.0 73.3 jit_solution(7561177400258409599)
XLA Ops:
  0.6 1.3 %broadcast_in_dim.6 = bf16[8,32,128]{2,1,0:T(8,128)(2,1)} broadcast(bf16[32,128]{1,0:T(8,128)(2,1)} %param.5), dimensions={1,2} | broadcast | bytes 73728 | tf_op jit(solution)/shard_map/broadcast_in_dim | solution.py:359
  2.0 10.9 %all-to-all-start.1 = ((bf16[8,32,128]{2,1,0:T(8,128)(2,1)}), bf16[8,32,128]{2,1,0:T(8,128)(2,1)S(1)}, u32[]{:S(2)}, u32[]{:S(2)}) async-start(bf16[8,32,128]{2,1,0:T(8,128)(2,1)} %broadcast_in_dim.6), calls=%async_computation.1 | async-start | bytes 131072 | tf_op jit(solution)/shard_map/all_to_all | solution.py:353
  12.8 2.1 %shard_map.68 = bf16[64,16,128]{2,1,0:T(8,128)(2,1)} custom-call(s32[32,128]{1,0:T(8,128)} %bitcast.7, bf16[64,1024]{1,0:T(8,128)(2,1)} %bitcast.6), custom_call_target="tpu_custom_call" | custom-call | tf_op jit(solution)/shard_map/pallas_call | solution.py:42
  15.0 5.1 %all-to-all-done.1.own_hbm = bf16[8,32,128]{2,1,0:T(8,128)(2,1)S(1)} async-done(((bf16[8,32,128]{2,1,0:T(8,128)(2,1)}), bf16[8,32,128]{2,1,0:T(8,128)(2,1)S(1)}, u32[]{:S(2)}, u32[]{:S(2)}) %all-to-all-start.1) | async-done | bytes 65568 | tf_op jit(solution)/shard_map/all_to_all | solution.py:353
  20.1 0.0 copy-start
  20.1 12.2 %all-to-all-start = ((bf16[64,16,128]{2,1,0:T(8,128)(2,1)}), bf16[64,16,128]{2,1,0:T(8,128)(2,1)S(1)}, u32[]{:S(2)}, u32[]{:S(2)}) async-start(bf16[64,16,128]{2,1,0:T(8,128)(2,1)} %shard_map.68), calls=%async_computation | async-start | bytes 524288 | tf_op jit(solution)/shard_map/all_to_all | solution.py:353
  32.3 3.5 %collective-permute-start = (bf16[8,32,128]{2,1,0:T(8,128)(2,1)S(1)}, bf16[8,32,128]{2,1,0:T(8,128)(2,1)S(1)}, u32[]{:S(2)}, u32[]{:S(2)}) collective-permute-start(bf16[8,32,128]{2,1,0:T(8,128)(2,1)S(1)} %all-to-all-done.1.own_hbm), channel_id=1, source_target_pairs={{1,2},{2,1},{3,4},{4,3},{5,6},{6,5},{7,8},{8,7},{9,10},{10,9},{11,... | collective-permute-start | bytes 196616 | tf_op jit(solution)/shard_map/ppermute | solution.py:375
  35.8 1.9 %collective-permute-start.1 = (bf16[8,32,128]{2,1,0:T(8,128)(2,1)S(1)}, bf16[8,32,128]{2,1,0:T(8,128)(2,1)S(1)}, u32[]{:S(2)}, u32[]{:S(2)}) collective-permute-start(bf16[8,32,128]{2,1,0:T(8,128)(2,1)S(1)} %all-to-all-done.1.own_hbm), channel_id=1, source_target_pairs={{0,1},{1,0},{2,3},{3,2},{4,5},{5,4},{6,7},{7,6},{8,9},{9,8},{10,11... | collective-permute-start | bytes 196616 | tf_op jit(solution)/shard_map/ppermute | solution.py:376
  37.8 2.0 %shard_map.69 = (bf16[6,256,512]{2,1,0:T(8,128)(2,1)S(1)}, bf16[24,256,256]{2,1,0:T(8,128)(2,1)S(1)}, bf16[4,32,128]{2,1,0:T(8,128)(2,1)S(1)}) custom-call(bf16[21,45]{1,0:T(8,128)(2,1)} %bitcast.9, bf16[21,45]{1,0:T(8,128)(2,1)} %bitcast.10, s32[32,128]{1,0:T(8,128)} %bitcast.8), custom_call_target="tpu_custom_call" | custom-call | tf_op jit(solution)/shard_map/pallas_call | solution.py:42
  39.7 0.0 collective-permute-done.far_ref
  39.7 0.0 collective-permute-done.1.near_ref
  39.7 0.0 copy-done
  39.7 6.5 %shard_map.70.basis_ref = bf16[8,1584,128]{2,1,0:T(8,128)(2,1)S(1)} custom-call(bf16[8,32,128]{2,1,0:T(8,128)(2,1)} %copy-done, bf16[8,32,128]{2,1,0:T(8,128)(2,1)S(1)} %collective-permute-done.far_ref, bf16[8,32,128]{2,1,0:T(8,128)(2,1)S(1)} %collective-permute-done.1.near_ref, bf16[6,256,512]{2,1,0:T(8,128)(2,1)S(1)} %get-tuple-element.9.row_band_ref, ...), custom_call_target="tpu_custom_call" | custom-call | tf_op jit(solution)/shard_map/pallas_call | solution.py:42
  46.2 0.0 all-to-all-done.got_ref
  46.2 1.0 %shard_map.71 = (f32[32,1024]{1,0:T(8,128)}, f32[8,16,128]{2,1,0:T(8,128)S(1)}) custom-call(bf16[64,16,128]{2,1,0:T(8,128)(2,1)S(1)} %all-to-all-done.got_ref, bf16[8,1584,128]{2,1,0:T(8,128)(2,1)S(1)} %shard_map.70.basis_ref), custom_call_target="tpu_custom_call" | custom-call | tf_op jit(solution)/shard_map/pallas_call | solution.py:42
  47.2 10.0 %all_to_all.20 = f32[8,16,128]{2,1,0:T(8,128)S(1)} all-to-all(f32[8,16,128]{2,1,0:T(8,128)S(1)} %get-tuple-element.13), channel_id=1, replica_groups=mesh['visit'=8,'y'=8,'x'=4,'core'=2] {'x','core'}, dimensions={0} | all-to-all | bytes 131072 | tf_op jit(solution)/shard_map/all_to_all | solution.py:353
  57.3 13.6 %all_to_all.21.parts_ref = f32[8,16,128]{2,1,0:T(8,128)S(1)} all-to-all(f32[8,16,128]{2,1,0:T(8,128)S(1)} %broadcast_in_dim.7), channel_id=1, replica_groups=mesh['visit'=8,'y'=8,'x'=4,'core'=2] {'y'}, dimensions={0} | all-to-all | bytes 131072 | tf_op jit(solution)/shard_map/all_to_all | solution.py:353
  70.9 2.4 %shard_map.72 = (f32[32,1024]{1,0:T(8,128)}, f32[1,128]{1,0:T(1,128)}) custom-call(f32[32,1024]{1,0:T(8,128)} %get-tuple-element.12.science_hbm, f32[8,16,128]{2,1,0:T(8,128)S(1)} %all_to_all.21.parts_ref, bf16[8,1584,128]{2,1,0:T(8,128)(2,1)S(1)} %shard_map.70.basis_ref), custom_call_target="tpu_custom_call" | custom-call | tf_op jit(solution)/shard_map/pallas_call | solution.py:42
  (2 shorter events, 0.0 us)
Async XLA Ops:
  2.0 18.1 %all-to-all-start.1 = ((bf16[8,32,128]{2,1,0:T(8,128)(2,1)}), bf16[8,32,128]{2,1,0:T(8,128)(2,1)S(1)}, u32[]{:S(2)}, u32[]{:S(2)}) async-start(bf16[8,32,128]{2,1,0:T(8,128)(2,1)} %broadcast_in_dim.6), calls=%async_computation.1 | async-start | bytes 131072 | tf_op jit(solution)/shard_map/all_to_all | solution.py:353
  20.1 19.7 %copy-start = (bf16[8,32,128]{2,1,0:T(8,128)(2,1)}, bf16[8,32,128]{2,1,0:T(8,128)(2,1)S(1)}, u32[]{:S(2)}) copy-start(bf16[8,32,128]{2,1,0:T(8,128)(2,1)S(1)} %all-to-all-done.1.own_hbm) | copy-start | bytes 196612
  20.1 26.2 %all-to-all-start = ((bf16[64,16,128]{2,1,0:T(8,128)(2,1)}), bf16[64,16,128]{2,1,0:T(8,128)(2,1)S(1)}, u32[]{:S(2)}, u32[]{:S(2)}) async-start(bf16[64,16,128]{2,1,0:T(8,128)(2,1)} %shard_map.68), calls=%async_computation | async-start | bytes 524288 | tf_op jit(solution)/shard_map/all_to_all | solution.py:353
  32.3 7.4 %collective-permute-start = (bf16[8,32,128]{2,1,0:T(8,128)(2,1)S(1)}, bf16[8,32,128]{2,1,0:T(8,128)(2,1)S(1)}, u32[]{:S(2)}, u32[]{:S(2)}) collective-permute-start(bf16[8,32,128]{2,1,0:T(8,128)(2,1)S(1)} %all-to-all-done.1.own_hbm), channel_id=1, source_target_pairs={{1,2},{2,1},{3,4},{4,3},{5,6},{6,5},{7,8},{8,7},{9,10},{10,9},{11,... | collective-permute-start | bytes 196616 | tf_op jit(solution)/shard_map/ppermute | solution.py:375
  35.8 3.9 %collective-permute-start.1 = (bf16[8,32,128]{2,1,0:T(8,128)(2,1)S(1)}, bf16[8,32,128]{2,1,0:T(8,128)(2,1)S(1)}, u32[]{:S(2)}, u32[]{:S(2)}) collective-permute-start(bf16[8,32,128]{2,1,0:T(8,128)(2,1)S(1)} %all-to-all-done.1.own_hbm), channel_id=1, source_target_pairs={{0,1},{1,0},{2,3},{3,2},{4,5},{5,4},{6,7},{7,6},{8,9},{9,8},{10,11... | collective-permute-start | bytes 196616 | tf_op jit(solution)/shard_map/ppermute | solution.py:376

commit v5 on v4

--- a/solution.py
+++ b/solution.py
@@ -19,7 +19,7 @@
 FRAME = ROWS + 2 * HALO
 OCT = 8
 OCTS = PAD // OCT
-SPAN = 16
+SPAN = 32
 SUB = 8
 TILE = 16
 AHEAD = 8
@@ -110,10 +110,14 @@
 
 
 def bands_kernel(
-    row_hbm, col_hbm, targets_hbm, row_band_ref, col_band_ref, hit_ref,
+    row_hbm, col_hbm, targets_hbm, own_hbm, row_band_ref, col_band_ref, hit_ref, own_ref,
     row_ref, col_ref, targets_ref, spread_ref, sems,
 ):
-    for copy in fetch([(row_hbm, row_ref), (col_hbm, col_ref), (targets_hbm, targets_ref)], sems):
+    copies = fetch(
+        [(row_hbm, row_ref), (col_hbm, col_ref), (targets_hbm, targets_ref), (own_hbm, own_ref)],
+        sems,
+    )
+    for copy in copies:
         copy.wait()
     hits(targets_ref, hit_ref)
     bands(row_ref, col_ref, row_band_ref, col_band_ref, spread_ref)
@@ -150,13 +154,11 @@
 
 
 def basis_kernel(
-    own_hbm, far_ref, near_ref, row_band_ref, col_band_ref, hit_ref,
-    basis_ref, own_ref, win_ref, even_ref, odd_ref, wide_ref, sems,
+    own_ref, far_ref, near_ref, row_band_ref, col_band_ref, hit_ref,
+    basis_ref, win_ref, even_ref, odd_ref, wide_ref,
 ):
-    copies = fetch([(own_hbm, own_ref)], sems)
     for i in range(4):
         basis_ref[1 + i, ROWS * PAD:ROWS * PAD + STRIPS // 2, :] = hit_ref[i]
-    copies[0].wait()
     first = lax.axis_index("core") == 0
     zero = jnp.zeros((FRAME, LANES // 2), BF16)
     halves = [zero]
@@ -374,40 +376,38 @@
     incoming = share(outgoing, STRIP)
     far_tiles = lax.ppermute(tiles, STRIP, outer)
     near_tiles = lax.ppermute(tiles, STRIP, inner)
-    row_bands, col_bands, hit = call(
+    row_bands, col_bands, hit, own = call(
         bands_kernel,
-        [((OCTS, OCT * ROWS, OCT * FRAME), BF16), ((PAD // 2, 2 * LANES, 2 * LANES), BF16), ((4, STRIPS // 2, LANES), BF16)],
+        [((OCTS, OCT * ROWS, OCT * FRAME), BF16), ((PAD // 2, 2 * LANES, 2 * LANES), BF16), ((4, STRIPS // 2, LANES), BF16), (tiles.shape, BF16)],
         row_taps.T,
         col_taps.T,
         targets,
+        tiles,
         scratch=[
             pltpu.VMEM((TAPS, NB), BF16),
             pltpu.VMEM((TAPS, NB), BF16),
             pltpu.VMEM(targets.shape, jnp.int32),
             pltpu.VMEM((LANES, LANES), F32),
-            pltpu.SemaphoreType.DMA((3,)),
+            pltpu.SemaphoreType.DMA((4,)),
         ],
-        far=3,
+        far=4,
     )
     (basis,) = call(
         basis_kernel,
         [((VISITS, ROWS * PAD + 3 * TILE, LANES), BF16)],
-        tiles,
+        own,
         far_tiles,
         near_tiles,
         row_bands,
         col_bands,
         hit,
         scratch=[
-            pltpu.VMEM((VISITS, ROWS, LANES), BF16),
             pltpu.VMEM((VISITS * FRAME, 2 * LANES), BF16),
             pltpu.VMEM((OCT * FRAME, COLS), BF16),
             pltpu.VMEM((OCT * FRAME, COLS), BF16),
             pltpu.VMEM((VISITS, ROWS * PAD, LANES), F32),
-            pltpu.SemaphoreType.DMA((1,)),
         ],
         grant=24,
-        far=1,
     )
     science, part = call(
         moment_kernel,

time: 74 us -> 74.4 us (level)
  transfers between devices with their start and end apart: 4 -> 4, of which waited for: 1 -> 1; matrix products, arithmetic and copies ran while one was open for 0% -> 0% of each run, Pallas kernels for 14% -> 15%
where the time goes in v5:
time: 74.4 us; the launch traced here: 73.8 us
  starting transfers between devices  28.5 us (38%)
  blocking collectives  23.5 us (32%)
  Pallas kernels  14.6 us (20%)
  waiting for transfers between devices  5.12 us (7%)
  local copies, waits for them, and re-layouts  1.35 us (2%)
    all_to_all x2, blocking collectives, share(): return lax.all_to_all(block, axis, 0, 0, tiled=True)  23.5 us
    all_to_all x2, starting transfers between devices, share(): return lax.all_to_all(block, axis, 0, 0, tiled=True)  23.1 us
    pallas_call x5, Pallas kernels, call(): pl.pallas_call(kernel, out_shape=tuple((pltpu.HBM(*o) if i < stay else ja...  14.6 us
    all_to_all x2, waiting for transfers between devices, share(): return lax.all_to_all(block, axis, 0, 0, tiled=True)  5.12 us
    ppermute x1, starting transfers between devices, body(): far_tiles = lax.ppermute(tiles, STRIP, outer)  3.54 us
    ppermute x1, starting transfers between devices, body(): near_tiles = lax.ppermute(tiles, STRIP, inner)  1.92 us
  transfers between devices with their start and end apart: 4, of which 1 were waited for; matrix products, arithmetic and copies ran while one was open for 0% of the time, Pallas kernels for 15%

profile of v5, /device:TPU:1, one launch (start us, length us, event | category | flops | bytes accessed | tf_op | source)
XLA Modules:
  0.0 73.8 jit_solution(18439001193709473143)
XLA Ops:
  0.6 1.3 %broadcast_in_dim.6 = bf16[8,32,128]{2,1,0:T(8,128)(2,1)} broadcast(bf16[32,128]{1,0:T(8,128)(2,1)} %param.5), dimensions={1,2} | broadcast | bytes 73728 | tf_op jit(solution)/shard_map/broadcast_in_dim | solution.py:361
  2.0 10.9 %all-to-all-start.1 = ((bf16[8,32,128]{2,1,0:T(8,128)(2,1)}), bf16[8,32,128]{2,1,0:T(8,128)(2,1)S(1)}, u32[]{:S(2)}, u32[]{:S(2)}) async-start(bf16[8,32,128]{2,1,0:T(8,128)(2,1)} %broadcast_in_dim.6), calls=%async_computation.1 | async-start | bytes 131072 | tf_op jit(solution)/shard_map/all_to_all | solution.py:355
  12.8 2.1 %shard_map.68 = bf16[64,16,128]{2,1,0:T(8,128)(2,1)} custom-call(s32[32,128]{1,0:T(8,128)} %bitcast.7, bf16[64,1024]{1,0:T(8,128)(2,1)} %bitcast.6), custom_call_target="tpu_custom_call" | custom-call | tf_op jit(solution)/shard_map/pallas_call | solution.py:42
  15.0 5.1 %all-to-all-done.1.own_hbm = bf16[8,32,128]{2,1,0:T(8,128)(2,1)S(1)} async-done(((bf16[8,32,128]{2,1,0:T(8,128)(2,1)}), bf16[8,32,128]{2,1,0:T(8,128)(2,1)S(1)}, u32[]{:S(2)}, u32[]{:S(2)}) %all-to-all-start.1) | async-done | bytes 65568 | tf_op jit(solution)/shard_map/all_to_all | solution.py:355
  20.1 0.0 copy-start
  20.1 12.2 %all-to-all-start = ((bf16[64,16,128]{2,1,0:T(8,128)(2,1)}), bf16[64,16,128]{2,1,0:T(8,128)(2,1)S(1)}, u32[]{:S(2)}, u32[]{:S(2)}) async-start(bf16[64,16,128]{2,1,0:T(8,128)(2,1)} %shard_map.68), calls=%async_computation | async-start | bytes 524288 | tf_op jit(solution)/shard_map/all_to_all | solution.py:355
  32.3 3.5 %collective-permute-start = (bf16[8,32,128]{2,1,0:T(8,128)(2,1)S(1)}, bf16[8,32,128]{2,1,0:T(8,128)(2,1)S(1)}, u32[]{:S(2)}, u32[]{:S(2)}) collective-permute-start(bf16[8,32,128]{2,1,0:T(8,128)(2,1)S(1)} %all-to-all-done.1.own_hbm), channel_id=1, source_target_pairs={{1,2},{2,1},{3,4},{4,3},{5,6},{6,5},{7,8},{8,7},{9,10},{10,9},{11,... | collective-permute-start | bytes 196616 | tf_op jit(solution)/shard_map/ppermute | solution.py:377
  35.8 1.9 %collective-permute-start.1 = (bf16[8,32,128]{2,1,0:T(8,128)(2,1)S(1)}, bf16[8,32,128]{2,1,0:T(8,128)(2,1)S(1)}, u32[]{:S(2)}, u32[]{:S(2)}) collective-permute-start(bf16[8,32,128]{2,1,0:T(8,128)(2,1)S(1)} %all-to-all-done.1.own_hbm), channel_id=1, source_target_pairs={{0,1},{1,0},{2,3},{3,2},{4,5},{5,4},{6,7},{7,6},{8,9},{9,8},{10,11... | collective-permute-start | bytes 196616 | tf_op jit(solution)/shard_map/ppermute | solution.py:378
  37.8 0.0 copy-done
  37.8 2.1 %shard_map.69 = (bf16[6,256,512]{2,1,0:T(8,128)(2,1)S(1)}, bf16[24,256,256]{2,1,0:T(8,128)(2,1)S(1)}, bf16[4,32,128]{2,1,0:T(8,128)(2,1)S(1)}, bf16[8,32,128]{2,1,0:T(8,128)(2,1)S(1)}) custom-call(bf16[21,45]{1,0:T(8,128)(2,1)} %bitcast.9, bf16[21,45]{1,0:T(8,128)(2,1)} %bitcast.10, s32[32,128]{1,0:T(8,128)} %bitcast.8, bf16[8,32,128]{2,1,0:T(8,128)(2,1)} %copy-done), custom_call_target="tpu_custom_call" | custom-call | tf_op jit(solution)/shard_map/pallas_call | solution.py:42
  39.9 0.0 collective-permute-done.far_ref
  39.9 0.0 collective-permute-done.1.near_ref
  39.9 6.9 %shard_map.70.basis_ref = bf16[8,1584,128]{2,1,0:T(8,128)(2,1)S(1)} custom-call(bf16[8,32,128]{2,1,0:T(8,128)(2,1)S(1)} %get-tuple-element.10.own_ref, bf16[8,32,128]{2,1,0:T(8,128)(2,1)S(1)} %collective-permute-done.far_ref, bf16[8,32,128]{2,1,0:T(8,128)(2,1)S(1)} %collective-permute-done.1.near_ref, ...), custom_call_target="tpu_custom_call" | custom-call | tf_op jit(solution)/shard_map/pallas_call | solution.py:42
  46.8 0.0 all-to-all-done.got_ref
  46.8 1.0 %shard_map.71 = (f32[32,1024]{1,0:T(8,128)}, f32[8,16,128]{2,1,0:T(8,128)S(1)}) custom-call(bf16[64,16,128]{2,1,0:T(8,128)(2,1)S(1)} %all-to-all-done.got_ref, bf16[8,1584,128]{2,1,0:T(8,128)(2,1)S(1)} %shard_map.70.basis_ref), custom_call_target="tpu_custom_call" | custom-call | tf_op jit(solution)/shard_map/pallas_call | solution.py:42
  47.8 9.9 %all_to_all.20 = f32[8,16,128]{2,1,0:T(8,128)S(1)} all-to-all(f32[8,16,128]{2,1,0:T(8,128)S(1)} %get-tuple-element.15), channel_id=1, replica_groups=mesh['visit'=8,'y'=8,'x'=4,'core'=2] {'x','core'}, dimensions={0} | all-to-all | bytes 131072 | tf_op jit(solution)/shard_map/all_to_all | solution.py:355
  57.7 13.6 %all_to_all.21.parts_ref = f32[8,16,128]{2,1,0:T(8,128)S(1)} all-to-all(f32[8,16,128]{2,1,0:T(8,128)S(1)} %broadcast_in_dim.7), channel_id=1, replica_groups=mesh['visit'=8,'y'=8,'x'=4,'core'=2] {'y'}, dimensions={0} | all-to-all | bytes 131072 | tf_op jit(solution)/shard_map/all_to_all | solution.py:355
  71.3 2.4 %shard_map.72 = (f32[32,1024]{1,0:T(8,128)}, f32[1,128]{1,0:T(1,128)}) custom-call(f32[32,1024]{1,0:T(8,128)} %get-tuple-element.14.science_hbm, f32[8,16,128]{2,1,0:T(8,128)S(1)} %all_to_all.21.parts_ref, bf16[8,1584,128]{2,1,0:T(8,128)(2,1)S(1)} %shard_map.70.basis_ref), custom_call_target="tpu_custom_call" | custom-call | tf_op jit(solution)/shard_map/pallas_call | solution.py:42
  (2 shorter events, 0.0 us)
Async XLA Ops:
  2.0 18.1 %all-to-all-start.1 = ((bf16[8,32,128]{2,1,0:T(8,128)(2,1)}), bf16[8,32,128]{2,1,0:T(8,128)(2,1)S(1)}, u32[]{:S(2)}, u32[]{:S(2)}) async-start(bf16[8,32,128]{2,1,0:T(8,128)(2,1)} %broadcast_in_dim.6), calls=%async_computation.1 | async-start | bytes 131072 | tf_op jit(solution)/shard_map/all_to_all | solution.py:355
  20.1 17.7 %copy-start = (bf16[8,32,128]{2,1,0:T(8,128)(2,1)}, bf16[8,32,128]{2,1,0:T(8,128)(2,1)S(1)}, u32[]{:S(2)}) copy-start(bf16[8,32,128]{2,1,0:T(8,128)(2,1)S(1)} %all-to-all-done.1.own_hbm) | copy-start | bytes 196612
  20.1 26.7 %all-to-all-start = ((bf16[64,16,128]{2,1,0:T(8,128)(2,1)}), bf16[64,16,128]{2,1,0:T(8,128)(2,1)S(1)}, u32[]{:S(2)}, u32[]{:S(2)}) async-start(bf16[64,16,128]{2,1,0:T(8,128)(2,1)} %shard_map.68), calls=%async_computation | async-start | bytes 524288 | tf_op jit(solution)/shard_map/all_to_all | solution.py:355
  32.3 7.6 %collective-permute-start = (bf16[8,32,128]{2,1,0:T(8,128)(2,1)S(1)}, bf16[8,32,128]{2,1,0:T(8,128)(2,1)S(1)}, u32[]{:S(2)}, u32[]{:S(2)}) collective-permute-start(bf16[8,32,128]{2,1,0:T(8,128)(2,1)S(1)} %all-to-all-done.1.own_hbm), channel_id=1, source_target_pairs={{1,2},{2,1},{3,4},{4,3},{5,6},{6,5},{7,8},{8,7},{9,10},{10,9},{11,... | collective-permute-start | bytes 196616 | tf_op jit(solution)/shard_map/ppermute | solution.py:377
  35.8 4.1 %collective-permute-start.1 = (bf16[8,32,128]{2,1,0:T(8,128)(2,1)S(1)}, bf16[8,32,128]{2,1,0:T(8,128)(2,1)S(1)}, u32[]{:S(2)}, u32[]{:S(2)}) collective-permute-start(bf16[8,32,128]{2,1,0:T(8,128)(2,1)S(1)} %all-to-all-done.1.own_hbm), channel_id=1, source_target_pairs={{0,1},{1,0},{2,3},{3,2},{4,5},{5,4},{6,7},{7,6},{8,9},{9,8},{10,11... | collective-permute-start | bytes 196616 | tf_op jit(solution)/shard_map/ppermute | solution.py:378
